TPU v7x, 32 devices: a whole 2x2x4 slice. The times are simulated.
32 devices in a mesh: seq: 4 (over y, core), fsdp: 8 (over z, x).
Axes of the slice: x: 2, y: 2, z: 4, core: 2. Of those that a mesh axis runs over, the one named last changes fastest.
Arguments:
- tokens: bfloat16 [2, 8, 256, 1536], P(None, 'fsdp', 'seq'), may hold values from -6 to 6
- segments: int32 [2, 8, 256], P(None, 'fsdp'), may hold values from 0 to 3, never falling along the last dimension, each value on 1 to 128 neighbouring positions
- routes: int32 [2, 8, 256, 2], P(None, 'fsdp'), may hold values from 0 to 3, all different within a row; in each aligned block of 64 rows (0 to 63, 64 to 127, ..., all dimensions but the last counted through in order) at most 48 rows name the same one
- cotangent: bfloat16 [2, 8, 256, 1536], P(None, 'fsdp', 'seq'), may hold values from -6 to 6
- norm1: bfloat16 [1536], P('fsdp'), may hold values from 0.25 to 1.75
- w_query: bfloat16 [1536, 1536], P('fsdp', 'seq'), may hold values from -0.15625 to 0.15625
- w_key: bfloat16 [1536, 512], P('fsdp', 'seq'), may hold values from -0.15625 to 0.15625
- w_value: bfloat16 [1536, 512], P('fsdp', 'seq'), may hold values from -0.15625 to 0.15625
- w_out: bfloat16 [1536, 1536], P('seq', 'fsdp'), may hold values from -0.875 to 0.875
- norm2: bfloat16 [1536], P('fsdp'), may hold values from 0.25 to 1.75
- w_router: bfloat16 [1536, 4], P('fsdp'), may hold values from -0.21875 to 0.21875
- w_gate: bfloat16 [4, 1536, 1024], P(None, 'fsdp', 'seq'), may hold values from -0.15625 to 0.15625
- w_up: bfloat16 [4, 1536, 1024], P(None, 'fsdp', 'seq'), may hold values from -0.15625 to 0.15625
- w_down: bfloat16 [4, 1024, 1536], P(None, 'seq', 'fsdp'), may hold values from -0.1875 to 0.1875
Outputs:
- layer_out: bfloat16 [2, 8, 256, 1536], P(None, 'fsdp', 'seq')
- grad_input: float32 [2, 8, 256, 1536], P(None, 'fsdp', 'seq')
- grad_norm1: float32 [1536], P('fsdp')
- grad_query: float32 [1536, 1536], P('fsdp', 'seq')
- grad_key: float32 [1536, 512], P('fsdp', 'seq')
- grad_value: float32 [1536, 512], P('fsdp', 'seq')
- grad_out: float32 [1536, 1536], P('seq', 'fsdp')
- grad_norm2: float32 [1536], P('fsdp')
- grad_router: float32 [1536, 4], P('fsdp')
- grad_gate: float32 [4, 1536, 1024], P(None, 'fsdp', 'seq')
- grad_up: float32 [4, 1536, 1024], P(None, 'fsdp', 'seq')
- grad_down: float32 [4, 1024, 1536], P(None, 'seq', 'fsdp')
Inputs may be any that keep to these rules, and one draw needn't show every extreme that they name: `segments`: each sequence's ids never fall; each of the 4 ids has 1 to 128 positions, and one has exactly 128. `routes`: A token's two experts differ. Within the rows of one device (aligned blocks of 64 rows in the order micro-batch, sequence, position) no expert is named by more than 48 rows, and in some block one is named by exactly 48.
All inputs are finite; a program needn't handle non-finite values.
Results may differ from a plain program's by a relative error of at most 0.02.
Values may be sent and summed in bfloat16 or wider, within the bound.
No kernel may reach another device: no remote copies, remote signals or barrier semaphores. Data moves between devices by JAX's collectives and lax.ppermute only.
A program may use at most 320 MiB of HBM per device.

v0:
```python
import functools

import jax
import jax.numpy as jnp
from jax import lax
from jax.experimental import pallas as pl
from jax.experimental.pallas import tpu as pltpu
from jax.sharding import PartitionSpec as P


D = 1536
HEADS = 24
HEAD_DIM = 64
KV_HEADS = 8
EXPERTS = 4
GROUP = HEADS // KV_HEADS
SCALE = HEAD_DIM**-0.5
EPS = 1e-05
NEG = -1e30
BF = jnp.bfloat16
F32 = jnp.float32
LANES = 128
EXTRA = 16
PAIR = 2
TILE = 384

VMEM = pl.BlockSpec(memory_space=pltpu.VMEM)
SMEM = pl.BlockSpec(memory_space=pltpu.SMEM)
ANY = pl.BlockSpec(memory_space=pl.ANY)


def mm(a, b, dims=((1,), (0,))):
    return lax.dot_general(a, b, (dims, ((), ())), preferred_element_type=F32)


def move(value, axis, bit):
    return lax.ppermute(value, axis, [(i, i ^ bit) for i in range(lax.axis_size(axis))])


def move_both(value, seq_bit, fsdp_bit):
    n = lax.axis_size("fsdp")
    pairs = [
        (s * n + f, (s ^ seq_bit) * n + (f ^ fsdp_bit))
        for s in range(lax.axis_size("seq"))
        for f in range(n)
    ]
    return lax.ppermute(value, ("seq", "fsdp"), pairs)


def spread(mine, other, n):
    units = [None] * n
    units[0] = mine
    for d in sorted(range(2, n, 2), key=lambda d: (d & (d - 1) != 0, -d)):
        units[d] = move(other if d & PAIR else mine, "fsdp", d)
    for d in range(0, n, 2):
        units[d ^ 1] = move(units[d], "fsdp", 1)
    return units


def collect(even, odd, n):
    odd = move(odd, "fsdp", 1)
    sums = [even[i].astype(F32) + odd[i].astype(F32) for i in range(n // 2)]
    got = {0: sums[0]}
    for i in range(n // 2 - 1, 0, -1):
        got[2 * i] = move(sums[i].astype(BF), "fsdp", 2 * i)
    return got


def total(parts):
    out = parts[0].astype(F32)
    for part in parts[1:]:
        out = out + part.astype(F32)
    return out


def add(a, b):
    return (a.astype(F32) + b.astype(F32)).astype(BF)


def seq_gather(block):
    second = move(block, "seq", 2)
    first = move(block, "seq", 1)
    third = move(second, "seq", 1)
    return [block, first, second, third]


def seq_scatter(terms):
    third = move(terms[3], "seq", 1)
    second = move(add(terms[2], third), "seq", 2)
    first = move(terms[1], "seq", 1)
    return [terms[0], first, second]


BLOCKS = ((0, 0), (2, 0), (0, PAIR), (2, PAIR), (1, 0), (3, 0), (1, PAIR), (3, PAIR))


def wide_gather(block):
    pair = move(block, "fsdp", PAIR)
    far = move(block, "seq", 2)
    both = move(pair, "seq", 2)
    near = [block, far, pair, both]
    return near + [move(b, "seq", 1) for b in near]


def wide_scatter(near, away):
    away = move(away, "seq", 1)
    both = move_both(add(near[3], away[3]), 2, PAIR)
    pair = move(add(near[2], away[2]), "fsdp", PAIR)
    far = move(add(near[1], away[1]), "seq", 2)
    return [near, away, far, pair, both]


def call(kernel, outs, scratch, specs, args, flops, moved, out_specs=None, grid=()):
    return pl.pallas_call(
        kernel,
        grid=grid,
        in_specs=specs,
        out_specs=out_specs or [VMEM] * len(outs),
        out_shape=[jax.ShapeDtypeStruct(s, d) for s, d in outs],
        scratch_shapes=scratch,
        compiler_params=pltpu.CompilerParams(vmem_limit_bytes=56 * 2**20),
        cost_estimate=pl.CostEstimate(
            flops=int(flops), bytes_accessed=int(moved), transcendentals=0
        ),
    )(*args)


def normal(v):
    return v * lax.rsqrt(jnp.mean(v * v, axis=-1, keepdims=True) + EPS)


def rows_of(owners, k, rows):
    return pl.ds(pl.multiple_of(owners[k] * rows, 16), rows)


def slabs(ref, micro, rows):
    per = ref.shape[0] // 4
    return jnp.concatenate([ref[pl.ds(j * per + micro * rows, rows)] for j in range(4)], axis=0)


def softmax(query, key, bias):
    scores = mm(query, key, ((1,), (1,))) + bias
    raised = jnp.exp(scores - jnp.max(scores, axis=-1, keepdims=True))
    return raised * (1.0 / jnp.sum(raised, axis=-1, keepdims=True))


def attn_pack_kernel(q_ref, k_ref, v_ref, o_ref, one_ref, two_ref, router_ref, out_ref):
    chunk, at = q_ref.shape[0], 0
    for ref in (q_ref, k_ref, v_ref, o_ref):
        out_ref[:chunk, at : at + ref.shape[1]] = ref[...]
        at += ref.shape[1]
    rest = jnp.zeros((EXTRA - 2 - EXPERTS, chunk), F32)
    small = [one_ref[...].reshape(1, chunk), two_ref[...].reshape(1, chunk), router_ref[...]]
    out_ref[chunk:, :chunk] = jnp.concatenate([v.astype(F32) for v in small] + [rest], axis=0).astype(BF)


def expert_pack_kernel(side, gate_ref, up_ref, down_ref, mine_ref, other_ref):
    hidden = gate_ref.shape[2] // 2
    wide = EXPERTS * hidden
    for e in range(EXPERTS):
        down = down_ref[e]
        for half in range(2):
            at = slice(half * hidden, (half + 1) * hidden)
            to = slice(e * hidden, (e + 1) * hidden)

            def put(ref):
                ref[:, to] = gate_ref[e, :, at]
                ref[:, slice(wide + to.start, wide + to.stop)] = up_ref[e, :, at]
                ref[:, slice(2 * wide + to.start, 2 * wide + to.stop)] = down[:, at]

            pl.when(side[0] == half)(functools.partial(put, mine_ref))
            pl.when(side[0] != half)(functools.partial(put, other_ref))


def norm_kernel(x_ref, a_ref, b_ref, c_ref, gain_ref, h_ref, n_ref):
    h = total([x_ref[...], a_ref[...], b_ref[...], c_ref[...]])
    h_ref[...] = h
    n_ref[...] = (normal(h) * gain_ref[1:2]).astype(BF)


def norm_back(v, gain, upstream):
    factor = lax.rsqrt(jnp.mean(v * v, axis=-1, keepdims=True) + EPS)
    normed = v * factor
    scaled = upstream * gain
    back = factor * (scaled - normed * jnp.mean(scaled * normed, axis=-1, keepdims=True))
    return back, jnp.sum(upstream * normed, axis=0, keepdims=True)


def norm_back_kernel(near_ref, away_ref, a_ref, b_ref, c_ref, h_ref, dy_ref, gain_ref, dh_ref, da_ref, g_ref):
    dn2 = total([near_ref[0], away_ref[0], a_ref[...], b_ref[...], c_ref[...]])
    back, grad = norm_back(h_ref[...], gain_ref[1:2], dn2)
    dh = dy_ref[...].astype(F32) + back
    dh_ref[...] = dh
    da_ref[...] = dh.astype(BF)
    g_ref[...] = grad


def input_kernel(x_ref, a_ref, b_ref, c_ref, dh_ref, gain_ref, out_ref):
    dn1 = total([a_ref[...], b_ref[...], c_ref[...]])
    out_ref[...] = dh_ref[...] + norm_back(x_ref[...].astype(F32), gain_ref[0:1], dn1)[0]


def attend_kernel(n, heads, owners, *refs):
    x_refs, pieces, refs = refs[:4], refs[4 : 4 + n], refs[4 + n :]
    bias_ref, n1_ref, qkv_ref, mix_ref, small_ref, *refs = refs
    part_refs, (w, extra, sem) = refs[:4], refs[4:]
    chunk = D // n
    copies = []
    for k, piece in enumerate(pieces):
        copies.append(
            pltpu.make_async_copy(piece.at[:chunk], w.at[rows_of(owners, k, chunk)], sem.at[0, k])
        )
        copies.append(
            pltpu.make_async_copy(
                piece.at[chunk:, : extra.shape[2]], extra.at[owners[k]], sem.at[1, k]
            )
        )
    for copy in copies:
        copy.start()
    block = x_refs[0].shape[0]
    q_cols = heads * HEAD_DIM
    kv_cols = q_cols // GROUP
    qkv_cols = q_cols + 2 * kv_cols
    for copy in copies:
        copy.wait()
    small = jnp.concatenate([extra[j].astype(F32)[:, :chunk] for j in range(n)], axis=1)
    small_ref[...] = small
    gain = small[0:1]
    for j in range(4):
        n1_ref[j * block : (j + 1) * block] = (normal(x_refs[j][...].astype(F32)) * gain).astype(BF)
    qkv_ref[...] = mm(n1_ref[...], w[:, :qkv_cols]).astype(BF)
    micro, rows = bias_ref.shape[0], bias_ref.shape[1] // 4
    for m in range(micro):
        qkv = slabs(qkv_ref, m, rows)
        bias = bias_ref[m]
        mixed = []
        for head in range(heads):
            kv = head // GROUP
            key = qkv[:, q_cols + kv * HEAD_DIM : q_cols + (kv + 1) * HEAD_DIM]
            value = qkv[:, q_cols + kv_cols + kv * HEAD_DIM : q_cols + kv_cols + (kv + 1) * HEAD_DIM]
            query = qkv[:, head * HEAD_DIM : (head + 1) * HEAD_DIM] * BF(SCALE)
            mixed.append(mm(softmax(query, key, bias).astype(BF), value).astype(BF))
        mixed = jnp.concatenate(mixed, axis=1)
        for j in range(4):
            mix_ref[pl.ds(j * block + m * rows, rows)] = mixed[j * rows : (j + 1) * rows]
    for j in range(4):
        mixed = mix_ref[j * block : (j + 1) * block]
        part_refs[j][...] = mm(mixed, w[:, qkv_cols:], ((1,), (1,))).astype(BF)


def store_units(even_ref, odd_ref, mine, first, value):
    rows = even_ref.shape[1]
    flag = (mine & 1) == 1
    for i in range(value.shape[0] // (2 * rows)):
        a = value[2 * i * rows : (2 * i + 1) * rows]
        b = value[(2 * i + 1) * rows : (2 * i + 2) * rows]
        slot = (mine >> 1) ^ (first + i)
        even_ref[slot] = jnp.where(flag, b, a).astype(BF)
        odd_ref[slot] = jnp.where(flag, a, b).astype(BF)


def tiles(rows, body):
    per = TILE // (2 * rows)

    def step(i, carry):
        body(pl.ds(pl.multiple_of(i * TILE, TILE), TILE), i * per)
        return carry

    lax.fori_loop(0, D // TILE, step, 0)


def out_back_kernel(n, owners, mine, *refs):
    da_refs, pieces, refs = refs[:4], refs[4 : 4 + n], refs[4 + n :]
    mix_ref, do_ref, even_ref, odd_ref, w, da_all, sem = refs
    chunk, q_cols = D // n, mix_ref.shape[1]
    copies = [
        pltpu.make_async_copy(
            piece.at[:chunk, piece.shape[1] - q_cols :], w.at[rows_of(owners, k, chunk)], sem.at[k]
        )
        for k, piece in enumerate(pieces)
    ]
    for copy in copies:
        copy.start()
    block = da_refs[0].shape[0]
    for j in range(4):
        da_all[j * block : (j + 1) * block] = da_refs[j][...]

    def grads(at, first):
        store_units(even_ref, odd_ref, mine[0], first, mm(da_all[:, at], mix_ref[...], ((0,), (0,))))

    tiles(chunk, grads)
    for copy in copies:
        copy.wait()
    do_ref[...] = mm(da_all[...], w[...]).astype(BF)


def attend_back_kernel(n, heads, owners, mine, *refs):
    pieces, refs = refs[:n], refs[n:]
    n1_ref, qkv_ref, do_ref, bias_ref, d_ref, *unit_refs, gain_ref, w, sem = refs
    chunk, cols = D // n, w.shape[1]
    copies = [
        pltpu.make_async_copy(piece.at[:chunk, :cols], w.at[rows_of(owners, k, chunk)], sem.at[k])
        for k, piece in enumerate(pieces)
    ]
    for copy in copies:
        copy.start()
    q_cols = heads * HEAD_DIM
    kv_cols = q_cols // GROUP
    micro, rows = bias_ref.shape[0], bias_ref.shape[1] // 4
    block, length = n1_ref.shape[0] // 4, 4 * rows
    for m in range(micro):
        qkv = slabs(qkv_ref, m, rows)
        grad = slabs(do_ref, m, rows)
        bias = bias_ref[m]
        grad_query, grad_key, grad_value = [], [], []
        for kv in range(heads // GROUP):
            key = qkv[:, q_cols + kv * HEAD_DIM : q_cols + (kv + 1) * HEAD_DIM]
            value = qkv[:, q_cols + kv_cols + kv * HEAD_DIM : q_cols + kv_cols + (kv + 1) * HEAD_DIM]
            scaled = key * BF(SCALE)
            sum_key = jnp.zeros((length, HEAD_DIM), F32)
            sum_value = jnp.zeros((length, HEAD_DIM), F32)
            for head in range(kv * GROUP, (kv + 1) * GROUP):
                query = qkv[:, head * HEAD_DIM : (head + 1) * HEAD_DIM] * BF(SCALE)
                upstream = grad[:, head * HEAD_DIM : (head + 1) * HEAD_DIM]
                probs = softmax(query, key, bias)
                dp = mm(upstream, value, ((1,), (1,)))
                ds = (probs * (dp - jnp.sum(dp * probs, axis=-1, keepdims=True))).astype(BF)
                grad_query.append(mm(ds, scaled).astype(BF))
                sum_key += mm(ds, query, ((0,), (0,)))
                sum_value += mm(probs.astype(BF), upstream, ((0,), (0,)))
            grad_key.append(sum_key.astype(BF))
            grad_value.append(sum_value.astype(BF))
        whole = jnp.concatenate(grad_query + grad_key + grad_value, axis=1)
        for j in range(4):
            d_ref[pl.ds(j * block + m * rows, rows)] = whole[j * rows : (j + 1) * rows]

    for copy in copies:
        copy.wait()
    ones = jnp.ones((8, 2 * cols), BF)

    def grads(at, first):
        value = mm(n1_ref[:, at], d_ref[...], ((0,), (0,)))
        store_units(*unit_refs[:2], mine[0], first, value[:, :q_cols])
        store_units(*unit_refs[2:], mine[0], first, value[:, q_cols:])
        gain_ref[:, at] = mm(ones, split(value * w[at].astype(F32)), ((1,), (1,)))

    tiles(chunk, grads)


def input_grad_kernel(n, owners, *refs):
    pieces, refs = refs[:n], refs[n:]
    d_ref, *refs = refs
    part_refs, (w, sem) = refs[:4], refs[4:]
    chunk, cols = D // n, d_ref.shape[1]
    copies = [
        pltpu.make_async_copy(piece.at[:chunk, :cols], w.at[rows_of(owners, k, chunk)], sem.at[k])
        for k, piece in enumerate(pieces)
    ]
    for copy in copies:
        copy.start()
    for copy in copies:
        copy.wait()
    block = part_refs[0].shape[0]
    for j in range(4):
        part_refs[j][...] = mm(d_ref[j * block : (j + 1) * block], w[...], ((1,), (1,))).astype(BF)


def split(v):
    high = v.astype(BF)
    return jnp.concatenate([high, (v - high.astype(F32)).astype(BF)], axis=1)


ROWS = 256


def expert_kernel(n, owners, *refs):
    n2_refs, dy_refs, pieces, refs = refs[:8], refs[8:16], refs[16 : 16 + n], refs[16 + n :]
    router_ref, chosen_ref, zg_out, dgu_out, near_out, away_out, *refs = refs
    w, n2_all, dy_all, chosen_all, zg, dgu, part, wsem, tsem, csem, osem = refs
    count, wide = zg.shape
    block = n2_refs[0].shape[0]
    chunk = D // n
    per = ROWS // block
    steps = count // ROWS
    cut = 2 * wide + LANES

    def tile(i):
        return pl.ds(pl.multiple_of(i * ROWS, ROWS), ROWS)

    first = [pltpu.make_async_copy(router_ref, w.at[:, 2 * wide : cut], csem.at[0])]
    second = []
    for k, piece in enumerate(pieces):
        at = rows_of(owners, k, chunk)
        first.append(pltpu.make_async_copy(piece.at[:, : 2 * wide], w.at[at, : 2 * wide], wsem.at[0, k]))
        second.append(pltpu.make_async_copy(piece.at[:, 2 * wide :], w.at[at, cut:], wsem.at[1, k]))
    tokens = []
    for k in range(len(n2_refs)):
        at = pl.ds(k * block, block)
        tokens.append(pltpu.make_async_copy(n2_refs[k], n2_all.at[at], tsem.at[0, k]))
        tokens.append(pltpu.make_async_copy(dy_refs[k], dy_all.at[at], tsem.at[1, k]))
    tokens.append(pltpu.make_async_copy(chosen_ref, chosen_all, csem.at[1]))
    for copy in first + tokens[: 2 * per] + tokens[-1:] + second:
        copy.start()
    for copy in first + tokens[-1:] + second:
        copy.wait()
    for copy in tokens[2 * per : -1]:
        copy.start()
    lane = lax.broadcasted_iota(jnp.int32, (LANES, wide), 0)
    column = lax.broadcasted_iota(jnp.int32, (LANES, wide), 1)
    expand = (lane == column // (wide // EXPERTS)).astype(BF)
    expand_two = jnp.concatenate([expand, expand], axis=0)

    def out_copies(i, h):
        b = pl.ds(i * per, per)
        here = near_out if h == 0 else away_out
        there = pl.ds(i * per - h * 4, per)
        return [
            pltpu.make_async_copy(zg.at[tile(i)], zg_out.at[tile(i)], osem.at[0, i]),
            pltpu.make_async_copy(dgu.at[tile(i)], dgu_out.at[tile(i)], osem.at[1, i]),
            pltpu.make_async_copy(part.at[b], here.at[there], osem.at[2, i]),
        ]

    for i in range(steps):
        at = tile(i)
        for copy in tokens[2 * per * i : 2 * per * (i + 1)]:
            copy.wait()
        chosen = chosen_all[at] > 0
        big = mm(n2_all[at], w[:, :cut])
        dz = mm(dy_all[at], w[:, cut:])
        g, u = big[:, :wide], big[:, wide : 2 * wide]
        logits = jnp.where(chosen, big[:, 2 * wide :], 0.0)
        other = jnp.sum(logits, axis=-1, keepdims=True) - logits
        gating = jnp.where(chosen, 1.0 / (1.0 + jnp.exp(other - logits)), 0.0)
        weight = mm(split(gating), expand_two)
        sig = 0.5 * jnp.tanh(0.5 * g) + 0.5
        act = g * sig
        z = act * u
        zg[at] = (z * weight).astype(BF)
        dgate = jnp.where(chosen, mm((z * dz).astype(BF), expand, ((1,), (1,))), 0.0)
        dz = dz * weight
        dgu[at, :wide] = (dz * u * (sig + act * (1.0 - sig))).astype(BF)
        dgu[at, wide : 2 * wide] = (dz * act).astype(BF)
        dlogits = gating * (dgate - jnp.sum(gating * dgate, axis=-1, keepdims=True))
        dgu[at, 2 * wide :] = dlogits.astype(BF)
        dn2 = mm(dgu[at], w[:, :cut], ((1,), (1,)))
        for b in range(per):
            part[i * per + b] = dn2[b * block : (b + 1) * block].astype(BF)
        for copy in out_copies(i, i * 2 // steps):
            copy.start()
    for i in range(steps):
        for copy in out_copies(i, i * 2 // steps):
            copy.wait()


def down_grad_kernel(n, mine, *refs):
    dy_refs, (zg_ref, even_ref, odd_ref, dy_all, sem) = refs[:8], refs[8:]
    block = dy_refs[0].shape[0]
    copies = [
        pltpu.make_async_copy(ref, dy_all.at[pl.ds(k * block, block)], sem.at[k])
        for k, ref in enumerate(dy_refs)
    ]
    for copy in copies:
        copy.start()
    for copy in copies:
        copy.wait()

    def grads(at, first):
        store_units(even_ref, odd_ref, mine[0], first, mm(dy_all[:, at], zg_ref[...], ((0,), (0,))))

    tiles(D // n, grads)


def gate_grad_kernel(n, mine, *refs):
    n2_refs, refs = refs[:8], refs[8:]
    dgu_ref, gate_even, gate_odd, up_even, up_odd, router_ref, n2_all, sem = refs
    block = n2_refs[0].shape[0]
    copies = [
        pltpu.make_async_copy(ref, n2_all.at[pl.ds(k * block, block)], sem.at[k])
        for k, ref in enumerate(n2_refs)
    ]
    for copy in copies:
        copy.start()
    for copy in copies:
        copy.wait()
    wide = gate_even.shape[2]

    def grads(at, first):
        value = mm(n2_all[:, at], dgu_ref[...], ((0,), (0,)))
        store_units(gate_even, gate_odd, mine[0], first, value[:, :wide])
        store_units(up_even, up_odd, mine[0], first, value[:, wide : 2 * wide])
        router_ref[:, at] = value[:, 2 * wide :].T[:8]

    tiles(D // n, grads)


def expert_out_kernel(n, owners, *refs):
    pieces, (zg_ref, near_ref, away_ref, w, sem) = refs[:n], refs[n:]
    wide = zg_ref.shape[1]
    chunk = D // n
    copies = [
        pltpu.make_async_copy(piece.at[:, 2 * wide :], w.at[rows_of(owners, k, chunk)], sem.at[k])
        for k, piece in enumerate(pieces)
    ]
    for copy in copies:
        copy.start()
    for copy in copies:
        copy.wait()
    block = near_ref.shape[1]
    for h, ref in enumerate((near_ref, away_ref)):
        value = mm(zg_ref[pl.ds(h * 4 * block, 4 * block)], w[...], ((1,), (1,)))
        ref[...] = value.astype(BF).reshape(4, block, D)


def on_device(
    tokens, segments, routes, cotangent, norm1, w_query, w_key, w_value, w_out,
    norm2, w_router, w_gate, w_up, w_down,
):
    seq = lax.axis_index("seq")
    mine = lax.axis_index("fsdp")
    n = lax.axis_size("fsdp")
    parts = lax.axis_size("seq")
    owners = (mine ^ jnp.arange(n, dtype=jnp.int32)).astype(jnp.int32)
    me = mine.reshape(1).astype(jnp.int32)
    side = jnp.where(mine & PAIR, 1, 0)
    micro, rows = tokens.shape[0], tokens.shape[2]
    own = micro * rows
    count = parts * own
    chunk = w_query.shape[0]
    q_cols, kv_cols = w_query.shape[1], w_key.shape[1]
    qkv_cols = q_cols + 2 * kv_cols
    heads = q_cols // HEAD_DIM
    hidden = w_gate.shape[2] // 2
    wide = EXPERTS * hidden

    (attn,) = call(
        attn_pack_kernel, [((chunk + EXTRA, qkv_cols + q_cols), BF)], [], [VMEM] * 7,
        [w_query, w_key, w_value, w_out.T, norm1, norm2, w_router.T], 0, 1e6,
    )
    attn_w = spread(attn, attn, n)
    x_own = tokens.reshape(own, D)
    dy_own = cotangent.reshape(own, D)
    x_all = seq_gather(x_own)

    here, there = call(
        expert_pack_kernel, [((chunk, 3 * wide), BF)] * 2, [], [SMEM] + [VMEM] * 3,
        [side.reshape(1).astype(jnp.int32), w_gate, w_up, jnp.swapaxes(w_down, 1, 2)], 0, 3e6,
    )
    expert_w = spread(here, there, n)
    dy_all = wide_gather(dy_own)

    ids = seq ^ jnp.arange(parts, dtype=jnp.int32)
    places = (ids[:, None] * rows + jnp.arange(rows, dtype=jnp.int32)[None]).reshape(-1)
    seg = jnp.take(segments[:, 0].reshape(micro, parts, rows), ids, axis=1).reshape(micro, -1)
    allowed = (seg[:, :, None] == seg[:, None, :]) & (places[None, None, :] <= places[None, :, None])
    bias = jnp.where(allowed, 0.0, NEG).astype(F32)
    here = routes[:, 0].reshape(-1, LANES)
    both = jnp.stack([here, move(here, "fsdp", PAIR)]).reshape(2, micro, parts, rows, 2)
    route = jnp.stack([both[1 if k else 0][:, seq ^ j] for j, k in BLOCKS]).reshape(-1, 2)
    lane = jnp.arange(LANES, dtype=jnp.int32)
    chosen = ((route[:, :1] == lane) | (route[:, 1:] == lane)).astype(F32)

    dma = pltpu.SemaphoreType.DMA
    block = ((own, D), BF)
    n1, qkv, mixed, small, *part = call(
        functools.partial(attend_kernel, n, heads),
        [((count, D), BF), ((count, qkv_cols), BF), ((count, q_cols), BF), ((EXTRA, D), F32)] + [block] * 4,
        [pltpu.VMEM((D, qkv_cols + q_cols), BF), pltpu.VMEM((n, EXTRA, 2 * LANES), BF), dma((2, n))],
        [SMEM] + [VMEM] * 4 + [ANY] * n + [VMEM],
        [owners, *x_all, *attn_w, bias],
        6e9, 9e6,
    )
    router = jnp.pad(small[2:6].astype(BF), ((0, LANES - 4), (0, 0))).T
    h, n2_own = call(
        norm_kernel, [((own, D), F32), block], [], [VMEM] * 5,
        [x_own, *seq_scatter(part), small], 0, 3e6,
    )
    n2_all = wide_gather(n2_own)
    span = len(BLOCKS) * own
    four = ((4, own, D), BF)
    zg, dgu, near, away = call(
        functools.partial(expert_kernel, n),
        [((span, wide), BF), ((span, 2 * wide + LANES), BF), four, four],
        [
            pltpu.VMEM((D, 3 * wide + LANES), BF), pltpu.VMEM((span, D), BF), pltpu.VMEM((span, D), BF),
            pltpu.VMEM((span, LANES), F32), pltpu.VMEM((span, wide), BF),
            pltpu.VMEM((span, 2 * wide + LANES), BF), pltpu.VMEM((len(BLOCKS), own, D), BF),
            dma((2, n)), dma((2, len(BLOCKS))), dma((2,)), dma((3, span // ROWS)),
        ],
        [SMEM] + [ANY] * (18 + n),
        [owners, *n2_all, *dy_all, *expert_w, router, chosen],
        8e9, 18e6, [ANY] * 4,
    )
    units = ((n // 2, chunk, wide), BF)
    down_even, down_odd = call(
        functools.partial(down_grad_kernel, n),
        [units] * 2,
        [pltpu.VMEM((span, D), BF), dma((len(BLOCKS),))],
        [SMEM] + [ANY] * 8 + [VMEM],
        [me, *dy_all, zg],
        1.6e9, 6e6,
    )
    dn2 = wide_scatter(near, away)
    gate_even, gate_odd, up_even, up_odd, grad_router = call(
        functools.partial(gate_grad_kernel, n),
        [units] * 4 + [((8, D), F32)],
        [pltpu.VMEM((span, D), BF), dma((len(BLOCKS),))],
        [SMEM] + [ANY] * 8 + [VMEM],
        [me, *n2_all, dgu],
        3.5e9, 9e6,
    )

    def share(got):
        near = total([got[d] for d in got if not d & PAIR])
        pair = total([got[d] for d in got if d & PAIR])
        low = jnp.where(side == 0, near, pair).reshape(chunk, EXPERTS, hidden)
        high = jnp.where(side == 0, pair, near).reshape(chunk, EXPERTS, hidden)
        return jnp.swapaxes(jnp.concatenate([low, high], axis=2), 0, 1)

    got_down = collect(down_even, down_odd, n)
    got_gate = collect(gate_even, gate_odd, n)
    got_up = collect(up_even, up_odd, n)

    corner = pl.BlockSpec((1, own, D), lambda i: (0, 0, 0))
    dh, da, grad_norm2 = call(
        norm_back_kernel, [((own, D), F32), block, ((1, D), F32)], [], [corner] * 2 + [VMEM] * 6,
        [*dn2, h, dy_own, small], 0, 5e6, grid=(1,),
    )

    da = seq_gather(da)
    y_near, y_away = call(
        functools.partial(expert_out_kernel, n),
        [four, four],
        [pltpu.VMEM((D, wide), BF), dma((n,))],
        [SMEM] + [ANY] * n + [VMEM],
        [owners, *expert_w, zg],
        1.6e9, 6e6,
    )
    do, out_even, out_odd = call(
        functools.partial(out_back_kernel, n),
        [((count, q_cols), BF), ((n // 2, chunk, q_cols), BF), ((n // 2, chunk, q_cols), BF)],
        [pltpu.VMEM((D, q_cols), BF), pltpu.VMEM((count, D), BF), dma((n,))],
        [SMEM] * 2 + [VMEM] * 4 + [ANY] * n + [VMEM],
        [owners, me, *da, *attn_w, mixed],
        1.2e9, 4e6,
    )
    got_out = collect(out_even, out_odd, n)
    dqkv, q_even, q_odd, kv_even, kv_odd, grad_norm1 = call(
        functools.partial(attend_back_kernel, n, heads),
        [((count, qkv_cols), BF)] + [((n // 2, chunk, q_cols), BF)] * 2
        + [((n // 2, chunk, 2 * kv_cols), BF)] * 2 + [((8, D), F32)],
        [pltpu.VMEM((D, qkv_cols), BF), dma((n,))],
        [SMEM] * 2 + [ANY] * n + [VMEM] * 4,
        [owners, me, *attn_w, n1, qkv, do, bias],
        8e9, 5e6,
    )
    sum_q = total(list(collect(q_even, q_odd, n).values()))
    sum_kv = total(list(collect(kv_even, kv_odd, n).values()))
    part = call(
        functools.partial(input_grad_kernel, n),
        [block] * 4,
        [pltpu.VMEM((D, qkv_cols), BF), dma((n,))],
        [SMEM] + [ANY] * n + [VMEM],
        [owners, *attn_w, dqkv],
        1e9, 6e6,
    )
    got_down, got_gate, got_up, got_out, _ = lax.optimization_barrier(
        (got_down, got_gate, got_up, got_out, part[0])
    )
    sum_down = jnp.swapaxes(share(got_down), 1, 2)
    sum_gate, sum_up = share(got_gate), share(got_up)
    sum_out = total(list(got_out.values())).T
    (grad_input,) = call(
        input_kernel, [((own, D), F32)], [], [VMEM] * 6,
        [x_own, *seq_scatter(part), dh, small], 0, 3e6,
    )
    y_parts = wide_scatter(y_near, y_away)
    layer_out = total([h, y_parts[0][0], y_parts[1][0], *y_parts[2:]]).astype(BF)

    tiny = jnp.concatenate([grad_norm1[:1], grad_norm2, grad_router[:4], jnp.zeros((2, D), F32)], axis=0)
    for bit in range(n.bit_length() - 1):
        tiny = tiny + move(tiny, "fsdp", 1 << bit)
    tiny = lax.dynamic_slice_in_dim(tiny, mine * chunk, chunk, axis=1)
    for bit in (2, 1):
        tiny = tiny + move(tiny, "seq", bit)

    lead = (micro, 1, rows, D)
    return (
        layer_out.reshape(lead),
        grad_input.reshape(lead),
        tiny[0] / norm1.astype(F32),
        sum_q,
        sum_kv[:, :kv_cols],
        sum_kv[:, kv_cols:],
        sum_out,
        tiny[1],
        tiny[2:6].T,
        sum_gate,
        sum_up,
        sum_down,
    )


def solution(mesh):
    return jax.shard_map(
        on_device,
        mesh=mesh,
        in_specs=(
            P(None, "fsdp", "seq", None),
            P(None, "fsdp", None),
            P(None, "fsdp", None, None),
            P(None, "fsdp", "seq", None),
            P("fsdp"),
            P("fsdp", "seq"),
            P("fsdp", "seq"),
            P("fsdp", "seq"),
            P("seq", "fsdp"),
            P("fsdp"),
            P("fsdp", None),
            P(None, "fsdp", "seq"),
            P(None, "fsdp", "seq"),
            P(None, "seq", "fsdp"),
        ),
        out_specs=(
            P(None, "fsdp", "seq", None),
            P(None, "fsdp", "seq", None),
            P("fsdp"),
            P("fsdp", "seq"),
            P("fsdp", "seq"),
            P("fsdp", "seq"),
            P("seq", "fsdp"),
            P("fsdp"),
            P("fsdp", None),
            P(None, "fsdp", "seq"),
            P(None, "fsdp", "seq"),
            P(None, "seq", "fsdp"),
        ),
        check_vma=False,
    )
```

profile of v0, /device:TPU:0, one launch (start us, length us, event | category | flops | bytes accessed | tf_op | source)
XLA Modules:
  0.0 404.7 jit_solution(2138436394238705162)
XLA Ops:
  11.8 6.9 %collective-permute-done.1.refs_2_ = bf16[128,1536]{1,0:T(8,128)(2,1)} collective-permute-done((bf16[128,1536]{1,0:T(8,128)(2,1)}, bf16[128,1536]{1,0:T(8,128)(2,1)}, u32[]{:S(2)}, u32[]{:S(2)}) %collective-permute-start.1) | collective-permute-done | bytes 393248 | tf_op jit(solution)/shard_map/ppermute | solution.py:37
  25.6 12.0 %collective-permute-done.6.refs_8_.refs_4_ = bf16[208,1024]{1,0:T(8,128)(2,1)S(1)} collective-permute-done((bf16[208,1024]{1,0:T(8,128)(2,1)}, bf16[208,1024]{1,0:T(8,128)(2,1)S(1)}, u32[]{:S(2)}, u32[]{:S(2)}) %collective-permute-start.6) | collective-permute-done | bytes 426016 | tf_op jit(solution)/shard_map/ppermute | solution.py:37
  41.2 9.1 %collective-permute-done.7.refs_9_.refs_5_ = bf16[208,1024]{1,0:T(8,128)(2,1)S(1)} collective-permute-done((bf16[208,1024]{1,0:T(8,128)(2,1)S(1)}, bf16[208,1024]{1,0:T(8,128)(2,1)S(1)}, u32[]{:S(2)}, u32[]{:S(2)}) %collective-permute-start.7) | collective-permute-done | bytes 426016 | tf_op jit(solution)/shard_map/ppermute | solution.py:37
  50.3 6.2 %collective-permute-done.9.refs_11_.refs_7_ = bf16[208,1024]{1,0:T(8,128)(2,1)S(1)} collective-permute-done((bf16[208,1024]{1,0:T(8,128)(2,1)S(1)}, bf16[208,1024]{1,0:T(8,128)(2,1)S(1)}, u32[]{:S(2)}, u32[]{:S(2)}) %collective-permute-start.9) | collective-permute-done | bytes 426016 | tf_op jit(solution)/shard_map/ppermute | solution.py:37
  57.3 10.7 %shard_map.230 = (bf16[512,1536]{1,0:T(8,128)(2,1)}, bf16[512,640]{1,0:T(8,128)(2,1)}, bf16[512,384]{1,0:T(8,128)(2,1)}, f32[16,1536]{1,0:T(8,128)}, bf16[128,15...) custom-call(s32[8]{0:T(128)} %iota_xor_fusion.1.owners, ...), custom_call_target="tpu_custom_call" | custom-call | flops 6000000000 | bytes 9000000 | tf_op jit(solution)/shard_map/pallas_call | solution.py:114
  87.8 7.2 %collective-permute-done.12.c_ref = bf16[128,1536]{1,0:T(8,128)(2,1)S(1)} collective-permute-done((bf16[128,1536]{1,0:T(8,128)(2,1)S(1)}, bf16[128,1536]{1,0:T(8,128)(2,1)S(1)}, u32[]{:S(2)}, u32[]{:S(2)}) %collective-permute-start.12) | collective-permute-done | bytes 393248 | tf_op jit(solution)/shard_map/ppermute | solution.py:37
  99.2 35.6 %collective-permute-done.16.refs_20_.refs_4_ = bf16[192,1536]{1,0:T(8,128)(2,1)} collective-permute-done((bf16[192,1536]{1,0:T(8,128)(2,1)}, bf16[192,1536]{1,0:T(8,128)(2,1)}, u32[]{:S(2)}, u32[]{:S(2)}) %collective-permute-start.16) | collective-permute-done | bytes 589856 | tf_op jit(solution)/shard_map/ppermute | solution.py:37
  139.2 8.7 %collective-permute-done.21.refs_2_ = bf16[128,1536]{1,0:T(8,128)(2,1)} collective-permute-done((bf16[128,1536]{1,0:T(8,128)(2,1)}, bf16[128,1536]{1,0:T(8,128)(2,1)}, u32[]{:S(2)}, u32[]{:S(2)}) %collective-permute-start.21) | collective-permute-done | bytes 393248 | tf_op jit(solution)/shard_map/ppermute | solution.py:37
  153.2 11.0 %collective-permute-done.15.refs_19_.refs_3_ = bf16[192,1536]{1,0:T(8,128)(2,1)S(1)} collective-permute-done((bf16[192,1536]{1,0:T(8,128)(2,1)S(1)}, bf16[192,1536]{1,0:T(8,128)(2,1)S(1)}, u32[]{:S(2)}, u32[]{:S(2)}) %collective-permute-start.15) | collective-permute-done | bytes 589856 | tf_op jit(solution)/shard_map/ppermute | solution.py:37
  167.9 8.2 %collective-permute-done.19.refs_23_.refs_7_ = bf16[192,1536]{1,0:T(8,128)(2,1)} collective-permute-done((bf16[192,1536]{1,0:T(8,128)(2,1)S(1)}, bf16[192,1536]{1,0:T(8,128)(2,1)}, u32[]{:S(2)}, u32[]{:S(2)}) %collective-permute-start.19) | collective-permute-done | bytes 589856 | tf_op jit(solution)/shard_map/ppermute | solution.py:37
  176.2 16.7 %shard_map.233 = (bf16[1024,512]{1,0:T(8,128)(2,1)}, bf16[1024,1152]{1,0:T(8,128)(2,1)}, bf16[4,128,1536]{2,1,0:T(8,128)(2,1)}, bf16[4,128,1536]{2,1,0:T(8,128)(2,1)}) custom-call(s32[8]{0:T(128)} %iota_xor_fusion.1.owners, bf16[128,1536]{1,0:T(8,128)(2,1)} %get-tuple-element.77.refs_0_, bf16[128,1536]{1,0:T(8,128)(2,1)} %collective-permute-done.20.refs_1_, ...), custom_call_target="tpu_custom_call" | custom-call | flops 8000000000 | bytes 18000000 | tf_op jit(solution)/shard_map/pallas_call | solution.py:114
  202.3 9.8 %shard_map.240 = (bf16[4,192,512]{2,1,0:T(8,128)(2,1)}, bf16[4,192,512]{2,1,0:T(8,128)(2,1)}, bf16[4,192,512]{2,1,0:T(8,128)(2,1)}, bf16[4,192,512]{2,1,0:T(8,128)(2,1)}, f32[8,1536]{1,0:T(8,128)}) custom-call(s32[1]{0:T(128)} %bitcast.26.mine, bf16[128,1536]{1,0:T(8,128)(2,1)} %get-tuple-element.77.refs_0_, ...), custom_call_target="tpu_custom_call" | custom-call | flops 3500000000 | bytes 9000000 | tf_op jit(solution)/shard_map/pallas_call | solution.py:114
  213.7 5.9 %collective-permute-done.42.c_ref = bf16[128,1536]{1,0:T(8,128)(2,1)S(1)} collective-permute-done((bf16[128,1536]{1,0:T(8,128)(2,1)S(1)}, bf16[128,1536]{1,0:T(8,128)(2,1)S(1)}, u32[]{:S(2)}, u32[]{:S(2)}) %collective-permute-start.42) | collective-permute-done | bytes 393248 | tf_op jit(solution)/shard_map/ppermute | solution.py:47
  227.0 5.8 %shard_map.234 = (bf16[4,128,1536]{2,1,0:T(8,128)(2,1)}, bf16[4,128,1536]{2,1,0:T(8,128)(2,1)}) custom-call(s32[8]{0:T(128)} %iota_xor_fusion.1.owners, bf16[192,1536]{1,0:T(8,128)(2,1)} %get-tuple-element.75.refs_16_.refs_0_, bf16[192,1536]{1,0:T(8,128)(2,1)} %collective-permute-done.13.refs_17_.refs_1_, bf16[192,1536]{1,0:T(8,128)(2,1)} %copy-done.33, ...), custom_call_target="tpu_custom_call" | custom-call | flops 1600000000 | bytes 6000000 | tf_op jit(solution)/shard_map/pallas_call | solution.py:114
  234.1 6.9 %shard_map.241 = (bf16[4,192,512]{2,1,0:T(8,128)(2,1)}, bf16[4,192,512]{2,1,0:T(8,128)(2,1)}) custom-call(s32[1]{0:T(128)} %bitcast.26.mine, bf16[128,1536]{1,0:T(8,128)(2,1)} %bitcast.180, bf16[128,1536]{1,0:T(8,128)(2,1)} %collective-permute-done.27.refs_9_.refs_1_, bf16[128,1536]{1,0:T(8,128)(2,1)} %collective-permute-done.28.refs_10_.refs_2_, ...), custom_call_target="tpu_custom_call" | custom-call | flops 1600000000 | bytes 6000000 | tf_op jit(solution)/shard_map/pallas_call | solution.py:114
  248.8 13.8 %shard_map.237 = (bf16[512,640]{1,0:T(8,128)(2,1)}, bf16[4,192,384]{2,1,0:T(8,128)(2,1)}, bf16[4,192,384]{2,1,0:T(8,128)(2,1)}, bf16[4,192,256]{2,1,0:T(8,128)(2...) custom-call(s32[8]{0:T(128)} %iota_xor_fusion.1.owners, s32[1]{0:T(128)} %bitcast.26.mine, ...), custom_call_target="tpu_custom_call" | custom-call | flops 8000000000 | bytes 5000000 | tf_op jit(solution)/shard_map/pallas_call | solution.py:114
  271.0 15.0 %collective-permute-done.50 = f32[8,1536]{1,0:T(8,128)S(1)} collective-permute-done((f32[8,1536]{1,0:T(8,128)S(1)}, f32[8,1536]{1,0:T(8,128)S(1)}, u32[]{:S(2)}, u32[]{:S(2)}) %collective-permute-start.50) | collective-permute-done | bytes 49184 | tf_op jit(solution)/shard_map/ppermute | solution.py:37
  295.7 6.2 %shard_map.238 = (bf16[128,1536]{1,0:T(8,128)(2,1)}, bf16[128,1536]{1,0:T(8,128)(2,1)}, bf16[128,1536]{1,0:T(8,128)(2,1)}, bf16[128,1536]{1,0:T(8,128)(2,1)}) custom-call(s32[8]{0:T(128)} %iota_xor_fusion.1.owners, bf16[208,1024]{1,0:T(8,128)(2,1)} %shard_map.229.refs_4_.refs_0_, bf16[208,1024]{1,0:T(8,128)(2,1)} %copy-done.5, bf16[208,1024]{1,0:T(8,128)(2,1)} %copy-done.2, ...), custom_call_target="tpu_custom_call" | custom-call | flops 1000000000 | bytes 6000000 | tf_op jit(solution)/shard_map/pallas_call | solution.py:114
  304.2 9.9 %collective-permute-done.58 = bf16[4,192,256]{2,1,0:T(8,128)(2,1)S(1)} collective-permute-done((bf16[4,192,256]{2,1,0:T(8,128)(2,1)S(1)}, bf16[4,192,256]{2,1,0:T(8,128)(2,1)S(1)}, u32[]{:S(2)}, u32[]{:S(2)}) %collective-permute-start.58) | collective-permute-done | bytes 393248 | tf_op jit(solution)/shard_map/ppermute | solution.py:37
  320.7 6.8 %collective-permute-start.72 = (bf16[192,512]{1,0:T(8,128)(2,1)S(1)}, bf16[192,512]{1,0:T(8,128)(2,1)S(1)}, u32[]{:S(2)}, u32[]{:S(2)}) collective-permute-start(bf16[192,512]{1,0:T(8,128)(2,1)S(1)} %get-tuple-element.169), channel_id=1, source_target_pairs={{0,4},{1,5},{2,6},{3,7},{4,0},{5,1},{6,2},{7,3},{8,12},{9,13},{10,... | collective-permute-start | bytes 589832 | tf_op jit(solution)/shard_map/ppermute | solution.py:37
  334.5 8.2 %collective-permute-done.72 = bf16[192,512]{1,0:T(8,128)(2,1)S(1)} collective-permute-done((bf16[192,512]{1,0:T(8,128)(2,1)S(1)}, bf16[192,512]{1,0:T(8,128)(2,1)S(1)}, u32[]{:S(2)}, u32[]{:S(2)}) %collective-permute-start.72) | collective-permute-done | bytes 196640 | tf_op jit(solution)/shard_map/ppermute | solution.py:37
  350.7 11.0 %collective-permute-done.68 = bf16[192,512]{1,0:T(8,128)(2,1)S(1)} collective-permute-done((bf16[192,512]{1,0:T(8,128)(2,1)S(1)}, bf16[192,512]{1,0:T(8,128)(2,1)S(1)}, u32[]{:S(2)}, u32[]{:S(2)}) %collective-permute-start.68) | collective-permute-done | bytes 196640 | tf_op jit(solution)/shard_map/ppermute | solution.py:37
  369.0 9.6 %collective-permute-done.64 = bf16[192,512]{1,0:T(8,128)(2,1)S(1)} collective-permute-done((bf16[192,512]{1,0:T(8,128)(2,1)S(1)}, bf16[192,512]{1,0:T(8,128)(2,1)S(1)}, u32[]{:S(2)}, u32[]{:S(2)}) %collective-permute-start.64) | collective-permute-done | bytes 196640 | tf_op jit(solution)/shard_map/ppermute | solution.py:37
  382.6 8.1 %collective-permute-done.76 = bf16[192,384]{1,0:T(8,128)(2,1)S(1)} collective-permute-done((bf16[192,384]{1,0:T(8,128)(2,1)S(1)}, bf16[192,384]{1,0:T(8,128)(2,1)S(1)}, u32[]{:S(2)}, u32[]{:S(2)}) %collective-permute-start.76) | collective-permute-done | bytes 147488 | tf_op jit(solution)/shard_map/ppermute | solution.py:37
  (311 shorter events, 153.5 us)
Async XLA Ops:
  5.6 32.1 %collective-permute-start.6 = (bf16[208,1024]{1,0:T(8,128)(2,1)}, bf16[208,1024]{1,0:T(8,128)(2,1)S(1)}, u32[]{:S(2)}, u32[]{:S(2)}) collective-permute-start(bf16[208,1024]{1,0:T(8,128)(2,1)} %shard_map.229.refs_4_.refs_0_), channel_id=1, source_target_pairs={{0,4},{1,5},{2,6},{3,7},{4,0},{5,1},{6,2},{7,3},{8,12},{9,13},{10,... | collective-permute-start | bytes 1277960 | tf_op jit(solution)/shard_map/ppermute | solution.py:37
  8.2 31.0 %collective-permute-start.8 = (bf16[208,1024]{1,0:T(8,128)(2,1)}, bf16[208,1024]{1,0:T(8,128)(2,1)S(1)}, u32[]{:S(2)}, u32[]{:S(2)}) collective-permute-start(bf16[208,1024]{1,0:T(8,128)(2,1)} %shard_map.229.refs_4_.refs_0_), channel_id=1, source_target_pairs={{0,6},{1,7},{2,4},{3,5},{4,2},{5,3},{6,0},{7,1},{8,14},{9,15},{10,... | collective-permute-start | bytes 1277960 | tf_op jit(solution)/shard_map/ppermute | solution.py:37
  79.8 54.9 %collective-permute-start.14 = (bf16[192,1536]{1,0:T(8,128)(2,1)}, bf16[192,1536]{1,0:T(8,128)(2,1)S(1)}, u32[]{:S(2)}, u32[]{:S(2)}) collective-permute-start(bf16[192,1536]{1,0:T(8,128)(2,1)} %get-tuple-element.76), channel_id=1, source_target_pairs={{0,2},{1,3},{2,0},{3,1},{4,6},{5,7},{6,4},{7,5},{8,10},{9,11},{10,... | collective-permute-start | bytes 1769480 | tf_op jit(solution)/shard_map/ppermute | solution.py:37
  80.2 55.1 %collective-permute-start.18 = (bf16[192,1536]{1,0:T(8,128)(2,1)}, bf16[192,1536]{1,0:T(8,128)(2,1)S(1)}, u32[]{:S(2)}, u32[]{:S(2)}) collective-permute-start(bf16[192,1536]{1,0:T(8,128)(2,1)} %get-tuple-element.76), channel_id=1, source_target_pairs={{0,6},{1,7},{2,4},{3,5},{4,2},{5,3},{6,0},{7,1},{8,14},{9,15},{10,... | collective-permute-start | bytes 1769480 | tf_op jit(solution)/shard_map/ppermute | solution.py:37
  83.4 51.4 %collective-permute-start.16 = (bf16[192,1536]{1,0:T(8,128)(2,1)}, bf16[192,1536]{1,0:T(8,128)(2,1)}, u32[]{:S(2)}, u32[]{:S(2)}) collective-permute-start(bf16[192,1536]{1,0:T(8,128)(2,1)} %get-tuple-element.75.refs_16_.refs_0_), channel_id=1, source_target_pairs={{0,4},{1,5},{2,6},{3,7},{4,0},{5,1},{6,2},{7,3},{8,12},{9,13},{10,... | collective-permute-start | bytes 1769480 | tf_op jit(solution)/shard_map/ppermute | solution.py:37
  83.7 53.0 %collective-permute-start.13 = (bf16[192,1536]{1,0:T(8,128)(2,1)}, bf16[192,1536]{1,0:T(8,128)(2,1)}, u32[]{:S(2)}, u32[]{:S(2)}) collective-permute-start(bf16[192,1536]{1,0:T(8,128)(2,1)} %get-tuple-element.75.refs_16_.refs_0_), channel_id=1, source_target_pairs={{0,1},{1,0},{2,3},{3,2},{4,5},{5,4},{6,7},{7,6},{8,9},{9,8},{10,11... | collective-permute-start | bytes 1769480 | tf_op jit(solution)/shard_map/ppermute | solution.py:37
  95.0 42.0 %collective-permute-start.29 = (bf16[128,1536]{1,0:T(8,128)(2,1)}, bf16[128,1536]{1,0:T(8,128)(2,1)}, u32[]{:S(2)}, u32[]{:S(2)}) collective-permute-start(bf16[128,1536]{1,0:T(8,128)(2,1)} %collective-permute-done.28.refs_10_.refs_2_), channel_id=1, source_target_pairs={{0,16},{8,24},{16,0},{24,8},{1,17},{9,25},{17,1},{25,9},{2,18},{10... | collective-permute-start | bytes 1179656 | tf_op jit(solution)/shard_map/ppermute | solution.py:37
  137.0 27.3 %collective-permute-start.15 = (bf16[192,1536]{1,0:T(8,128)(2,1)S(1)}, bf16[192,1536]{1,0:T(8,128)(2,1)S(1)}, u32[]{:S(2)}, u32[]{:S(2)}) collective-permute-start(bf16[192,1536]{1,0:T(8,128)(2,1)S(1)} %collective-permute-done.14.refs_18_.refs_2_), channel_id=1, source_target_pairs={{0,1},{1,0},{2,3},{3,2},{4,5},{5,4},{6,7},{7,6},{8,9},{9,8},{10,11... | collective-permute-start | bytes 1769480 | tf_op jit(solution)/shard_map/ppermute | solution.py:37
  137.6 26.7 %collective-permute-start.20 = (bf16[128,1536]{1,0:T(8,128)(2,1)}, bf16[128,1536]{1,0:T(8,128)(2,1)}, u32[]{:S(2)}, u32[]{:S(2)}) collective-permute-start(bf16[128,1536]{1,0:T(8,128)(2,1)} %get-tuple-element.77.refs_0_), channel_id=1, source_target_pairs={{0,16},{8,24},{16,0},{24,8},{1,17},{9,25},{17,1},{25,9},{2,18},{10... | collective-permute-start | bytes 1179656 | tf_op jit(solution)/shard_map/ppermute | solution.py:37
  151.7 24.5 %collective-permute-start.19 = (bf16[192,1536]{1,0:T(8,128)(2,1)S(1)}, bf16[192,1536]{1,0:T(8,128)(2,1)}, u32[]{:S(2)}, u32[]{:S(2)}) collective-permute-start(bf16[192,1536]{1,0:T(8,128)(2,1)S(1)} %collective-permute-done.18.refs_22_.refs_6_), channel_id=1, source_target_pairs={{0,1},{1,0},{2,3},{3,2},{4,5},{5,4},{6,7},{7,6},{8,9},{9,8},{10,11... | collective-permute-start | bytes 1769480 | tf_op jit(solution)/shard_map/ppermute | solution.py:37
  153.2 23.0 %collective-permute-start.23 = (bf16[128,1536]{1,0:T(8,128)(2,1)}, bf16[128,1536]{1,0:T(8,128)(2,1)}, u32[]{:S(2)}, u32[]{:S(2)}) collective-permute-start(bf16[128,1536]{1,0:T(8,128)(2,1)} %get-tuple-element.77.refs_0_), channel_id=1, source_target_pairs={{0,8},{8,0},{16,24},{24,16},{1,9},{9,1},{17,25},{25,17},{2,10},{10... | collective-permute-start | bytes 1179656 | tf_op jit(solution)/shard_map/ppermute | solution.py:37
  212.1 29.0 %collective-permute-start.70 = (bf16[4,192,512]{2,1,0:T(8,128)(2,1)}, bf16[4,192,512]{2,1,0:T(8,128)(2,1)S(1)}, u32[]{:S(2)}, u32[]{:S(2)}) collective-permute-start(bf16[4,192,512]{2,1,0:T(8,128)(2,1)} %get-tuple-element.107), channel_id=1, source_target_pairs={{0,1},{1,0},{2,3},{3,2},{4,5},{5,4},{6,7},{7,6},{8,9},{9,8},{10,11... | collective-permute-start | bytes 2359304 | tf_op jit(solution)/shard_map/ppermute | solution.py:37
  225.5 43.8 %collective-permute-start.66 = (bf16[4,192,512]{2,1,0:T(8,128)(2,1)}, bf16[4,192,512]{2,1,0:T(8,128)(2,1)S(1)}, u32[]{:S(2)}, u32[]{:S(2)}) collective-permute-start(bf16[4,192,512]{2,1,0:T(8,128)(2,1)} %get-tuple-element.105), channel_id=1, source_target_pairs={{0,1},{1,0},{2,3},{3,2},{4,5},{5,4},{6,7},{7,6},{8,9},{9,8},{10,11... | collective-permute-start | bytes 2359304 | tf_op jit(solution)/shard_map/ppermute | solution.py:37
  232.8 31.3 %collective-permute-start.35 = (bf16[4,128,1536]{2,1,0:T(8,128)(2,1)}, bf16[4,128,1536]{2,1,0:T(8,128)(2,1)S(1)}, u32[]{:S(2)}, u32[]{:S(2)}) collective-permute-start(bf16[4,128,1536]{2,1,0:T(8,128)(2,1)} %get-tuple-element.80), channel_id=1, source_target_pairs={{0,8},{8,0},{16,24},{24,16},{1,9},{9,1},{17,25},{25,17},{2,10},{10... | collective-permute-start | bytes 4718600 | tf_op jit(solution)/shard_map/ppermute | solution.py:37
  241.1 45.5 %collective-permute-start.62 = (bf16[4,192,512]{2,1,0:T(8,128)(2,1)}, bf16[4,192,512]{2,1,0:T(8,128)(2,1)S(1)}, u32[]{:S(2)}, u32[]{:S(2)}) collective-permute-start(bf16[4,192,512]{2,1,0:T(8,128)(2,1)} %get-tuple-element.103), channel_id=1, source_target_pairs={{0,1},{1,0},{2,3},{3,2},{4,5},{5,4},{6,7},{7,6},{8,9},{9,8},{10,11... | collective-permute-start | bytes 2359304 | tf_op jit(solution)/shard_map/ppermute | solution.py:37
  264.4 28.1 %collective-permute-start.36 = (bf16[128,1536]{1,0:T(8,128)(2,1)S(1)}, bf16[128,1536]{1,0:T(8,128)(2,1)S(1)}, u32[]{:S(2)}, u32[]{:S(2)}) collective-permute-start(bf16[128,1536]{1,0:T(8,128)(2,1)S(1)} %get-tuple-element.165), channel_id=1, source_target_pairs={{0,16},{8,24},{16,0},{24,8},{1,17},{9,25},{17,1},{25,9},{2,18},{10... | collective-permute-start | bytes 1179656 | tf_op jit(solution)/shard_map/ppermute | solution.py:37
  266.0 26.5 %collective-permute-start.37 = (bf16[128,1536]{1,0:T(8,128)(2,1)S(1)}, bf16[128,1536]{1,0:T(8,128)(2,1)S(1)}, u32[]{:S(2)}, u32[]{:S(2)}) collective-permute-start(bf16[128,1536]{1,0:T(8,128)(2,1)S(1)} %get-tuple-element.167), channel_id=1, source_target_pairs={{0,2},{1,3},{2,0},{3,1},{4,6},{5,7},{6,4},{7,5},{8,10},{9,11},{10,... | collective-permute-start | bytes 1179656 | tf_op jit(solution)/shard_map/ppermute | solution.py:37
  267.7 24.9 %collective-permute-start.38 = (bf16[128,1536]{1,0:T(8,128)(2,1)S(1)}, bf16[128,1536]{1,0:T(8,128)(2,1)S(1)}, u32[]{:S(2)}, u32[]{:S(2)}) collective-permute-start(bf16[128,1536]{1,0:T(8,128)(2,1)S(1)} %get-tuple-element.166), channel_id=1, source_target_pairs={{0,18},{1,19},{2,16},{3,17},{4,22},{5,23},{6,20},{7,21},{8,26},{9,... | collective-permute-start | bytes 1179656 | tf_op jit(solution)/shard_map/ppermute | solution.py:47
  286.0 48.5 %collective-permute-start.71 = (bf16[192,512]{1,0:T(8,128)(2,1)S(1)}, bf16[192,512]{1,0:T(8,128)(2,1)S(1)}, u32[]{:S(2)}, u32[]{:S(2)}) collective-permute-start(bf16[192,512]{1,0:T(8,128)(2,1)S(1)} %get-tuple-element.170), channel_id=1, source_target_pairs={{0,2},{1,3},{2,0},{3,1},{4,6},{5,7},{6,4},{7,5},{8,10},{9,11},{10,... | collective-permute-start | bytes 589832 | tf_op jit(solution)/shard_map/ppermute | solution.py:37
  293.6 51.5 %collective-permute-start.74 = (bf16[4,192,384]{2,1,0:T(8,128)(2,1)S(1)}, bf16[4,192,384]{2,1,0:T(8,128)(2,1)S(1)}, u32[]{:S(2)}, u32[]{:S(2)}) collective-permute-start(bf16[4,192,384]{2,1,0:T(8,128)(2,1)S(1)} %copy-done.36), channel_id=1, source_target_pairs={{0,1},{1,0},{2,3},{3,2},{4,5},{5,4},{6,7},{7,6},{8,9},{9,8},{10,11... | collective-permute-start | bytes 1769480 | tf_op jit(solution)/shard_map/ppermute | solution.py:37
  332.3 35.1 %collective-permute-start.54 = (bf16[4,192,384]{2,1,0:T(8,128)(2,1)S(1)}, bf16[4,192,384]{2,1,0:T(8,128)(2,1)S(1)}, u32[]{:S(2)}, u32[]{:S(2)}) collective-permute-start(bf16[4,192,384]{2,1,0:T(8,128)(2,1)S(1)} %copy-done.35), channel_id=1, source_target_pairs={{0,1},{1,0},{2,3},{3,2},{4,5},{5,4},{6,7},{7,6},{8,9},{9,8},{10,11... | collective-permute-start | bytes 1769480 | tf_op jit(solution)/shard_map/ppermute | solution.py:37
  350.6 28.0 %collective-permute-start.64 = (bf16[192,512]{1,0:T(8,128)(2,1)S(1)}, bf16[192,512]{1,0:T(8,128)(2,1)S(1)}, u32[]{:S(2)}, u32[]{:S(2)}) collective-permute-start(bf16[192,512]{1,0:T(8,128)(2,1)S(1)} %get-tuple-element.177), channel_id=1, source_target_pairs={{0,4},{1,5},{2,6},{3,7},{4,0},{5,1},{6,2},{7,3},{8,12},{9,13},{10,... | collective-permute-start | bytes 589832 | tf_op jit(solution)/shard_map/ppermute | solution.py:37
  366.5 24.2 %collective-permute-start.76 = (bf16[192,384]{1,0:T(8,128)(2,1)S(1)}, bf16[192,384]{1,0:T(8,128)(2,1)S(1)}, u32[]{:S(2)}, u32[]{:S(2)}) collective-permute-start(bf16[192,384]{1,0:T(8,128)(2,1)S(1)} %get-tuple-element.181), channel_id=1, source_target_pairs={{0,4},{1,5},{2,6},{3,7},{4,0},{5,1},{6,2},{7,3},{8,12},{9,13},{10,... | collective-permute-start | bytes 442376 | tf_op jit(solution)/shard_map/ppermute | solution.py:37
  367.4 23.3 %collective-permute-start.77 = (bf16[192,384]{1,0:T(8,128)(2,1)S(1)}, bf16[192,384]{1,0:T(8,128)(2,1)S(1)}, u32[]{:S(2)}, u32[]{:S(2)}) collective-permute-start(bf16[192,384]{1,0:T(8,128)(2,1)S(1)} %get-tuple-element.180), channel_id=1, source_target_pairs={{0,6},{1,7},{2,4},{3,5},{4,2},{5,3},{6,0},{7,1},{8,14},{9,15},{10,... | collective-permute-start | bytes 442376 | tf_op jit(solution)/shard_map/ppermute | solution.py:37
  (96 other events, 1351.3 us)
where the time goes:
time: 411 us; the launch traced here: 405 us
  waiting for transfers between devices  196 us (48%)
  starting transfers between devices  92.7 us (23%)
  Pallas kernels  88.9 us (22%)
  other arithmetic  14.7 us (4%)
  local copies, waits for them, and re-layouts  11 us (3%)
    ppermute x76, waiting for transfers between devices, move(): lax.ppermute(value, axis, [(i, i ^ bit) for i in range(lax.axis_size(axis...  190 us
    ppermute x76, starting transfers between devices, move(): lax.ppermute(value, axis, [(i, i ^ bit) for i in range(lax.axis_size(axis...  89.2 us
    pallas_call x13, Pallas kernels, call(): pl.pallas_call(kernel, grid=grid, in_specs=specs, out_specs=out_specs or...  88.9 us
  transfers between devices with their start and end apart: 78, of which 26 were waited for; matrix products, arithmetic and copies ran while one was open for 5% of the time, Pallas kernels for 14%

commit v1 on v0

--- a/solution.py
+++ b/solution.py
@@ -50,7 +50,7 @@
 def spread(mine, other, n):
     units = [None] * n
     units[0] = mine
-    for d in sorted(range(2, n, 2), key=lambda d: (d & (d - 1) != 0, -d)):
+    for d in directions(n):
         units[d] = move(other if d & PAIR else mine, "fsdp", d)
     for d in range(0, n, 2):
         units[d ^ 1] = move(units[d], "fsdp", 1)
@@ -133,9 +133,13 @@
     return pl.ds(pl.multiple_of(owners[k] * rows, 16), rows)
 
 
+def slab(j, per, micro, rows):
+    return pl.ds(pl.multiple_of(j * per + micro * rows, rows), rows)
+
+
 def slabs(ref, micro, rows):
     per = ref.shape[0] // 4
-    return jnp.concatenate([ref[pl.ds(j * per + micro * rows, rows)] for j in range(4)], axis=0)
+    return jnp.concatenate([ref[slab(j, per, micro, rows)] for j in range(4)], axis=0)
 
 
 def softmax(query, key, bias):
@@ -144,9 +148,9 @@
     return raised * (1.0 / jnp.sum(raised, axis=-1, keepdims=True))
 
 
-def attn_pack_kernel(q_ref, k_ref, v_ref, o_ref, one_ref, two_ref, router_ref, out_ref):
+def attn_pack_kernel(q_ref, k_ref, v_ref, one_ref, two_ref, router_ref, out_ref):
     chunk, at = q_ref.shape[0], 0
-    for ref in (q_ref, k_ref, v_ref, o_ref):
+    for ref in (q_ref, k_ref, v_ref):
         out_ref[:chunk, at : at + ref.shape[1]] = ref[...]
         at += ref.shape[1]
     rest = jnp.zeros((EXTRA - 2 - EXPERTS, chunk), F32)
@@ -200,37 +204,52 @@
     out_ref[...] = dh_ref[...] + norm_back(x_ref[...].astype(F32), gain_ref[0:1], dn1)[0]
 
 
-def attend_kernel(n, heads, owners, *refs):
-    x_refs, pieces, refs = refs[:4], refs[4 : 4 + n], refs[4 + n :]
-    bias_ref, n1_ref, qkv_ref, mix_ref, small_ref, *refs = refs
-    part_refs, (w, extra, sem) = refs[:4], refs[4:]
-    chunk = D // n
-    copies = []
-    for k, piece in enumerate(pieces):
-        copies.append(
-            pltpu.make_async_copy(piece.at[:chunk], w.at[rows_of(owners, k, chunk)], sem.at[0, k])
-        )
-        copies.append(
-            pltpu.make_async_copy(
-                piece.at[chunk:, : extra.shape[2]], extra.at[owners[k]], sem.at[1, k]
-            )
-        )
+def fetch(pieces, owners, whole, sem, rows, columns=slice(None)):
+    copies = [
+        pltpu.make_async_copy(piece.at[:rows, columns], whole.at[rows_of(owners, k, rows)], sem.at[k])
+        for k, piece in enumerate(pieces)
+    ]
     for copy in copies:
         copy.start()
-    block = x_refs[0].shape[0]
-    q_cols = heads * HEAD_DIM
-    kv_cols = q_cols // GROUP
-    qkv_cols = q_cols + 2 * kv_cols
+    return copies
+
+
+def wait(copies):
     for copy in copies:
         copy.wait()
+
+
+def qkv_kernel(n, owners, *refs):
+    x_refs, pieces, refs = refs[:4], refs[4 : 4 + n], refs[4 + n :]
+    n1_ref, qkv_ref, small_ref, w, extra, sem, small_sem = refs
+    chunk = D // n
+    smalls = [
+        pltpu.make_async_copy(piece.at[chunk:, : extra.shape[2]], extra.at[owners[k]], small_sem.at[k])
+        for k, piece in enumerate(pieces)
+    ]
+    for copy in smalls:
+        copy.start()
+    copies = fetch(pieces, owners, w, sem, chunk)
+    wait(smalls)
     small = jnp.concatenate([extra[j].astype(F32)[:, :chunk] for j in range(n)], axis=1)
     small_ref[...] = small
     gain = small[0:1]
+    block = x_refs[0].shape[0]
     for j in range(4):
         n1_ref[j * block : (j + 1) * block] = (normal(x_refs[j][...].astype(F32)) * gain).astype(BF)
-    qkv_ref[...] = mm(n1_ref[...], w[:, :qkv_cols]).astype(BF)
+    wait(copies)
+    qkv_ref[...] = mm(n1_ref[...], w[...]).astype(BF)
+
+
+def attend_kernel(n, heads, owners, *refs):
+    pieces, (qkv_ref, bias_ref, mix_ref, probs_ref, *part_refs, w, sem) = refs[:n], refs[n:]
+    copies = fetch(pieces, owners, w, sem, D // n)
+    q_cols = heads * HEAD_DIM
+    kv_cols = q_cols // GROUP
     micro, rows = bias_ref.shape[0], bias_ref.shape[1] // 4
-    for m in range(micro):
+    block = qkv_ref.shape[0] // 4
+
+    def sequence(m, carry):
         qkv = slabs(qkv_ref, m, rows)
         bias = bias_ref[m]
         mixed = []
@@ -239,24 +258,30 @@
             key = qkv[:, q_cols + kv * HEAD_DIM : q_cols + (kv + 1) * HEAD_DIM]
             value = qkv[:, q_cols + kv_cols + kv * HEAD_DIM : q_cols + kv_cols + (kv + 1) * HEAD_DIM]
             query = qkv[:, head * HEAD_DIM : (head + 1) * HEAD_DIM] * BF(SCALE)
-            mixed.append(mm(softmax(query, key, bias).astype(BF), value).astype(BF))
+            probs = softmax(query, key, bias).astype(BF)
+            probs_ref[m * heads + head] = probs
+            mixed.append(mm(probs, value).astype(BF))
         mixed = jnp.concatenate(mixed, axis=1)
         for j in range(4):
-            mix_ref[pl.ds(j * block + m * rows, rows)] = mixed[j * rows : (j + 1) * rows]
+            mix_ref[slab(j, block, m, rows)] = mixed[j * rows : (j + 1) * rows]
+        return carry
+
+    lax.fori_loop(0, micro, sequence, 0)
+    wait(copies)
+    part = mm(mix_ref[...], w[...], ((1,), (1,))).astype(BF)
     for j in range(4):
-        mixed = mix_ref[j * block : (j + 1) * block]
-        part_refs[j][...] = mm(mixed, w[:, qkv_cols:], ((1,), (1,))).astype(BF)
+        part_refs[j][...] = part[j * block : (j + 1) * block]
 
 
 def store_units(even_ref, odd_ref, mine, first, value):
-    rows = even_ref.shape[1]
+    rows = D // (2 * even_ref.shape[0])
     flag = (mine & 1) == 1
     for i in range(value.shape[0] // (2 * rows)):
         a = value[2 * i * rows : (2 * i + 1) * rows]
         b = value[(2 * i + 1) * rows : (2 * i + 2) * rows]
         slot = (mine >> 1) ^ (first + i)
-        even_ref[slot] = jnp.where(flag, b, a).astype(BF)
-        odd_ref[slot] = jnp.where(flag, a, b).astype(BF)
+        even_ref[slot, :rows] = jnp.where(flag, b, a).astype(BF)
+        odd_ref[slot, :rows] = jnp.where(flag, a, b).astype(BF)
 
 
 def tiles(rows, body):
@@ -272,15 +297,8 @@
 def out_back_kernel(n, owners, mine, *refs):
     da_refs, pieces, refs = refs[:4], refs[4 : 4 + n], refs[4 + n :]
     mix_ref, do_ref, even_ref, odd_ref, w, da_all, sem = refs
-    chunk, q_cols = D // n, mix_ref.shape[1]
-    copies = [
-        pltpu.make_async_copy(
-            piece.at[:chunk, piece.shape[1] - q_cols :], w.at[rows_of(owners, k, chunk)], sem.at[k]
-        )
-        for k, piece in enumerate(pieces)
-    ]
-    for copy in copies:
-        copy.start()
+    chunk = D // n
+    copies = fetch(pieces, owners, w, sem, chunk)
     block = da_refs[0].shape[0]
     for j in range(4):
         da_all[j * block : (j + 1) * block] = da_refs[j][...]
@@ -289,60 +307,68 @@
         store_units(even_ref, odd_ref, mine[0], first, mm(da_all[:, at], mix_ref[...], ((0,), (0,))))
 
     tiles(chunk, grads)
-    for copy in copies:
-        copy.wait()
+    wait(copies)
     do_ref[...] = mm(da_all[...], w[...]).astype(BF)
 
 
 def attend_back_kernel(n, heads, owners, mine, *refs):
     pieces, refs = refs[:n], refs[n:]
-    n1_ref, qkv_ref, do_ref, bias_ref, d_ref, *unit_refs, gain_ref, w, sem = refs
+    n1_ref, qkv_ref, do_ref, probs_ref, norm2_ref, router_ref, d_ref, *unit_refs, w, sem = refs
     chunk, cols = D // n, w.shape[1]
-    copies = [
-        pltpu.make_async_copy(piece.at[:chunk, :cols], w.at[rows_of(owners, k, chunk)], sem.at[k])
-        for k, piece in enumerate(pieces)
-    ]
-    for copy in copies:
-        copy.start()
+    copies = fetch(pieces, owners, w, sem, chunk)
     q_cols = heads * HEAD_DIM
     kv_cols = q_cols // GROUP
-    micro, rows = bias_ref.shape[0], bias_ref.shape[1] // 4
-    block, length = n1_ref.shape[0] // 4, 4 * rows
-    for m in range(micro):
+    block = n1_ref.shape[0] // 4
+    length = probs_ref.shape[1]
+    rows, micro = length // 4, probs_ref.shape[0] // heads
+
+    def sequence(m, carry):
         qkv = slabs(qkv_ref, m, rows)
         grad = slabs(do_ref, m, rows)
-        bias = bias_ref[m]
         grad_query, grad_key, grad_value = [], [], []
         for kv in range(heads // GROUP):
-            key = qkv[:, q_cols + kv * HEAD_DIM : q_cols + (kv + 1) * HEAD_DIM]
+            key = qkv[:, q_cols + kv * HEAD_DIM : q_cols + (kv + 1) * HEAD_DIM] * BF(SCALE)
             value = qkv[:, q_cols + kv_cols + kv * HEAD_DIM : q_cols + kv_cols + (kv + 1) * HEAD_DIM]
-            scaled = key * BF(SCALE)
             sum_key = jnp.zeros((length, HEAD_DIM), F32)
             sum_value = jnp.zeros((length, HEAD_DIM), F32)
             for head in range(kv * GROUP, (kv + 1) * GROUP):
                 query = qkv[:, head * HEAD_DIM : (head + 1) * HEAD_DIM] * BF(SCALE)
                 upstream = grad[:, head * HEAD_DIM : (head + 1) * HEAD_DIM]
-                probs = softmax(query, key, bias)
+                low = probs_ref[m * heads + head]
+                probs = low.astype(F32)
                 dp = mm(upstream, value, ((1,), (1,)))
                 ds = (probs * (dp - jnp.sum(dp * probs, axis=-1, keepdims=True))).astype(BF)
-                grad_query.append(mm(ds, scaled).astype(BF))
+                grad_query.append(mm(ds, key).astype(BF))
                 sum_key += mm(ds, query, ((0,), (0,)))
-                sum_value += mm(probs.astype(BF), upstream, ((0,), (0,)))
+                sum_value += mm(low, upstream, ((0,), (0,)))
             grad_key.append(sum_key.astype(BF))
             grad_value.append(sum_value.astype(BF))
         whole = jnp.concatenate(grad_query + grad_key + grad_value, axis=1)
         for j in range(4):
-            d_ref[pl.ds(j * block + m * rows, rows)] = whole[j * rows : (j + 1) * rows]
-
-    for copy in copies:
-        copy.wait()
+            d_ref[slab(j, block, m, rows)] = whole[j * rows : (j + 1) * rows]
+        return carry
+
+    lax.fori_loop(0, micro, sequence, 0)
+    wait(copies)
     ones = jnp.ones((8, 2 * cols), BF)
+    q_even, q_odd, kv_even, kv_odd = unit_refs
+    flag = (mine[0] & 1) == 1
 
     def grads(at, first):
         value = mm(n1_ref[:, at], d_ref[...], ((0,), (0,)))
-        store_units(*unit_refs[:2], mine[0], first, value[:, :q_cols])
-        store_units(*unit_refs[2:], mine[0], first, value[:, q_cols:])
-        gain_ref[:, at] = mm(ones, split(value * w[at].astype(F32)), ((1,), (1,)))
+        store_units(q_even, q_odd, mine[0], first, value[:, :q_cols])
+        store_units(kv_even, kv_odd, mine[0], first, value[:, q_cols:])
+        gain = mm(ones, split(value * w[at].astype(F32)), ((1,), (1,)))
+        small = [gain[:1], norm2_ref[:, at], router_ref[:EXPERTS, at]]
+        small.append(jnp.zeros((EXTRA - 2 - EXPERTS, TILE), F32))
+        small = jnp.concatenate(small, axis=0)
+        pad = jnp.zeros((EXTRA, q_cols - chunk), F32)
+        for i in range(TILE // (2 * chunk)):
+            a = small[:, 2 * i * chunk : (2 * i + 1) * chunk]
+            b = small[:, (2 * i + 1) * chunk : (2 * i + 2) * chunk]
+            slot = (mine[0] >> 1) ^ (first + i)
+            q_even[slot, chunk:] = jnp.concatenate([jnp.where(flag, b, a), pad], axis=1).astype(BF)
+            q_odd[slot, chunk:] = jnp.concatenate([jnp.where(flag, a, b), pad], axis=1).astype(BF)
 
     tiles(chunk, grads)
 
@@ -351,18 +377,11 @@
     pieces, refs = refs[:n], refs[n:]
     d_ref, *refs = refs
     part_refs, (w, sem) = refs[:4], refs[4:]
-    chunk, cols = D // n, d_ref.shape[1]
-    copies = [
-        pltpu.make_async_copy(piece.at[:chunk, :cols], w.at[rows_of(owners, k, chunk)], sem.at[k])
-        for k, piece in enumerate(pieces)
-    ]
-    for copy in copies:
-        copy.start()
-    for copy in copies:
-        copy.wait()
+    wait(fetch(pieces, owners, w, sem, D // n))
     block = part_refs[0].shape[0]
+    part = mm(d_ref[...], w[...], ((1,), (1,))).astype(BF)
     for j in range(4):
-        part_refs[j][...] = mm(d_ref[j * block : (j + 1) * block], w[...], ((1,), (1,))).astype(BF)
+        part_refs[j][...] = part[j * block : (j + 1) * block]
 
 
 def split(v):
@@ -373,9 +392,9 @@
 ROWS = 256
 
 
-def expert_kernel(n, owners, *refs):
+def expert_kernel(n, owners, mine, *refs):
     n2_refs, dy_refs, pieces, refs = refs[:8], refs[8:16], refs[16 : 16 + n], refs[16 + n :]
-    router_ref, chosen_ref, zg_out, dgu_out, near_out, away_out, *refs = refs
+    router_ref, chosen_ref, zg_out, dgu_out, near_out, away_out, even_ref, odd_ref, *refs = refs
     w, n2_all, dy_all, chosen_all, zg, dgu, part, wsem, tsem, csem, osem = refs
     count, wide = zg.shape
     block = n2_refs[0].shape[0]
@@ -396,34 +415,37 @@
     tokens = []
     for k in range(len(n2_refs)):
         at = pl.ds(k * block, block)
-        tokens.append(pltpu.make_async_copy(n2_refs[k], n2_all.at[at], tsem.at[0, k]))
-        tokens.append(pltpu.make_async_copy(dy_refs[k], dy_all.at[at], tsem.at[1, k]))
-    tokens.append(pltpu.make_async_copy(chosen_ref, chosen_all, csem.at[1]))
-    for copy in first + tokens[: 2 * per] + tokens[-1:] + second:
+        tokens.append(pltpu.make_async_copy(n2_refs[k], n2_all.at[at], tsem.at[0, k // per]))
+        tokens.append(pltpu.make_async_copy(dy_refs[k], dy_all.at[at], tsem.at[1, k // per]))
+    masks = pltpu.make_async_copy(chosen_ref, chosen_all, csem.at[1])
+    for copy in first + tokens[: 2 * per] + [masks] + second:
         copy.start()
-    for copy in first + tokens[-1:] + second:
+    for copy in first + [masks] + second:
         copy.wait()
-    for copy in tokens[2 * per : -1]:
+    for copy in tokens[2 * per :]:
         copy.start()
     lane = lax.broadcasted_iota(jnp.int32, (LANES, wide), 0)
     column = lax.broadcasted_iota(jnp.int32, (LANES, wide), 1)
     expand = (lane == column // (wide // EXPERTS)).astype(BF)
     expand_two = jnp.concatenate([expand, expand], axis=0)
 
-    def out_copies(i, h):
-        b = pl.ds(i * per, per)
-        here = near_out if h == 0 else away_out
-        there = pl.ds(i * per - h * 4, per)
+    half = steps // 2
+
+    def row_copies(i):
         return [
             pltpu.make_async_copy(zg.at[tile(i)], zg_out.at[tile(i)], osem.at[0, i]),
             pltpu.make_async_copy(dgu.at[tile(i)], dgu_out.at[tile(i)], osem.at[1, i]),
-            pltpu.make_async_copy(part.at[b], here.at[there], osem.at[2, i]),
         ]
 
-    for i in range(steps):
+    def part_copy(i, out, start):
+        return pltpu.make_async_copy(
+            part.at[pl.ds(i * per, per)], out.at[pl.ds(i * per - start, per)], osem.at[2, i]
+        )
+
+    def step(i, carry):
         at = tile(i)
-        for copy in tokens[2 * per * i : 2 * per * (i + 1)]:
-            copy.wait()
+        for which, ref in enumerate((n2_all, dy_all)):
+            pltpu.make_async_copy(ref.at[at], ref.at[at], tsem.at[which, i]).wait()
         chosen = chosen_all[at] > 0
         big = mm(n2_all[at], w[:, :cut])
         dz = mm(dy_all[at], w[:, cut:])
@@ -445,29 +467,22 @@
         dn2 = mm(dgu[at], w[:, :cut], ((1,), (1,)))
         for b in range(per):
             part[i * per + b] = dn2[b * block : (b + 1) * block].astype(BF)
-        for copy in out_copies(i, i * 2 // steps):
+        for copy in row_copies(i):
             copy.start()
+        pl.when(i < half)(lambda: part_copy(i, near_out, 0).start())
+        pl.when(i >= half)(lambda: part_copy(i, away_out, half * per).start())
+        return carry
+
+    lax.fori_loop(0, steps, step, 0)
+
+    def grads(at, first):
+        store_units(even_ref, odd_ref, mine[0], first, mm(dy_all[:, at], zg[...], ((0,), (0,))))
+
+    tiles(chunk, grads)
     for i in range(steps):
-        for copy in out_copies(i, i * 2 // steps):
+        for copy in row_copies(i):
             copy.wait()
-
-
-def down_grad_kernel(n, mine, *refs):
-    dy_refs, (zg_ref, even_ref, odd_ref, dy_all, sem) = refs[:8], refs[8:]
-    block = dy_refs[0].shape[0]
-    copies = [
-        pltpu.make_async_copy(ref, dy_all.at[pl.ds(k * block, block)], sem.at[k])
-        for k, ref in enumerate(dy_refs)
-    ]
-    for copy in copies:
-        copy.start()
-    for copy in copies:
-        copy.wait()
-
-    def grads(at, first):
-        store_units(even_ref, odd_ref, mine[0], first, mm(dy_all[:, at], zg_ref[...], ((0,), (0,))))
-
-    tiles(D // n, grads)
+        (part_copy(i, near_out, 0) if i < half else part_copy(i, away_out, half * per)).wait()
 
 
 def gate_grad_kernel(n, mine, *refs):
@@ -497,18 +512,25 @@
     pieces, (zg_ref, near_ref, away_ref, w, sem) = refs[:n], refs[n:]
     wide = zg_ref.shape[1]
     chunk = D // n
-    copies = [
-        pltpu.make_async_copy(piece.at[:, 2 * wide :], w.at[rows_of(owners, k, chunk)], sem.at[k])
-        for k, piece in enumerate(pieces)
-    ]
-    for copy in copies:
-        copy.start()
-    for copy in copies:
-        copy.wait()
+    wait(fetch(pieces, owners, w, sem, chunk, slice(2 * wide, 3 * wide)))
     block = near_ref.shape[1]
     for h, ref in enumerate((near_ref, away_ref)):
         value = mm(zg_ref[pl.ds(h * 4 * block, 4 * block)], w[...], ((1,), (1,)))
         ref[...] = value.astype(BF).reshape(4, block, D)
+
+
+def finish_kernel(counts, hidden, side, *refs):
+    ins, outs = refs[: sum(counts)], refs[sum(counts) :]
+    first = side[0] == 0
+    for count, out in zip(counts[:-1], outs):
+        here, ins = ins[:count], ins[count:]
+        near = total([ref[...] for ref in here[: count // 2]])
+        pair = total([ref[...] for ref in here[count // 2 :]])
+        for e in range(EXPERTS):
+            at = slice(e * hidden, (e + 1) * hidden)
+            out[e, :, :hidden] = jnp.where(first, near[:, at], pair[:, at])
+            out[e, :, hidden:] = jnp.where(first, pair[:, at], near[:, at])
+    outs[-1][...] = total([ref[...] for ref in ins])
 
 
 def on_device(
@@ -533,10 +555,11 @@
     wide = EXPERTS * hidden
 
     (attn,) = call(
-        attn_pack_kernel, [((chunk + EXTRA, qkv_cols + q_cols), BF)], [], [VMEM] * 7,
-        [w_query, w_key, w_value, w_out.T, norm1, norm2, w_router.T], 0, 1e6,
-    )
-    attn_w = spread(attn, attn, n)
+        attn_pack_kernel, [((chunk + EXTRA, qkv_cols), BF)], [], [VMEM] * 6,
+        [w_query, w_key, w_value, norm1, norm2, w_router.T], 0, 1e6,
+    )
+    qkv_w = spread(attn, attn, n)
+    out_w = spread(w_out.T, w_out.T, n)
     x_own = tokens.reshape(own, D)
     dy_own = cotangent.reshape(own, D)
     x_all = seq_gather(x_own)
@@ -561,14 +584,22 @@
 
     dma = pltpu.SemaphoreType.DMA
     block = ((own, D), BF)
-    n1, qkv, mixed, small, *part = call(
+    n1, qkv, small = call(
+        functools.partial(qkv_kernel, n),
+        [((count, D), BF), ((count, qkv_cols), BF), ((EXTRA, D), F32)],
+        [pltpu.VMEM((D, qkv_cols), BF), pltpu.VMEM((n, EXTRA, 2 * LANES), BF), dma((n,)), dma((n,))],
+        [SMEM] + [VMEM] * 4 + [ANY] * n,
+        [owners, *x_all, *qkv_w],
+        1e9, 6e6,
+    )
+    length = parts * rows
+    mixed, probs, *part = call(
         functools.partial(attend_kernel, n, heads),
-        [((count, D), BF), ((count, qkv_cols), BF), ((count, q_cols), BF), ((EXTRA, D), F32)] + [block] * 4,
-        [pltpu.VMEM((D, qkv_cols + q_cols), BF), pltpu.VMEM((n, EXTRA, 2 * LANES), BF), dma((2, n))],
-        [SMEM] + [VMEM] * 4 + [ANY] * n + [VMEM],
-        [owners, *x_all, *attn_w, bias],
-        6e9, 9e6,
-    )
+        [((count, q_cols), BF), ((micro * heads, length, length), BF)] + [block] * 4,
+        [pltpu.VMEM((D, q_cols), BF), dma((n,))],
+        [SMEM] + [ANY] * n + [VMEM] * 2, [owners, *out_w, qkv, bias], 5e9, 6e6,
+    )
+
     router = jnp.pad(small[2:6].astype(BF), ((0, LANES - 4), (0, 0))).T
     h, n2_own = call(
         norm_kernel, [((own, D), F32), block], [], [VMEM] * 5,
@@ -577,27 +608,19 @@
     n2_all = wide_gather(n2_own)
     span = len(BLOCKS) * own
     four = ((4, own, D), BF)
-    zg, dgu, near, away = call(
+    units = ((n // 2, chunk, wide), BF)
+    zg, dgu, near, away, down_even, down_odd = call(
         functools.partial(expert_kernel, n),
-        [((span, wide), BF), ((span, 2 * wide + LANES), BF), four, four],
+        [((span, wide), BF), ((span, 2 * wide + LANES), BF), four, four, units, units],
         [
             pltpu.VMEM((D, 3 * wide + LANES), BF), pltpu.VMEM((span, D), BF), pltpu.VMEM((span, D), BF),
             pltpu.VMEM((span, LANES), F32), pltpu.VMEM((span, wide), BF),
             pltpu.VMEM((span, 2 * wide + LANES), BF), pltpu.VMEM((len(BLOCKS), own, D), BF),
-            dma((2, n)), dma((2, len(BLOCKS))), dma((2,)), dma((3, span // ROWS)),
+            dma((2, n)), dma((2, span // ROWS)), dma((2,)), dma((3, span // ROWS)),
         ],
-        [SMEM] + [ANY] * (18 + n),
-        [owners, *n2_all, *dy_all, *expert_w, router, chosen],
-        8e9, 18e6, [ANY] * 4,
-    )
-    units = ((n // 2, chunk, wide), BF)
-    down_even, down_odd = call(
-        functools.partial(down_grad_kernel, n),
-        [units] * 2,
-        [pltpu.VMEM((span, D), BF), dma((len(BLOCKS),))],
-        [SMEM] + [ANY] * 8 + [VMEM],
-        [me, *dy_all, zg],
-        1.6e9, 6e6,
+        [SMEM] * 2 + [ANY] * (18 + n),
+        [owners, me, *n2_all, *dy_all, *expert_w, router, chosen],
+        1e10, 2e7, [ANY] * 4 + [VMEM] * 2,
     )
     dn2 = wide_scatter(near, away)
     gate_even, gate_odd, up_even, up_odd, grad_router = call(
@@ -609,13 +632,6 @@
         3.5e9, 9e6,
     )
 
-    def share(got):
-        near = total([got[d] for d in got if not d & PAIR])
-        pair = total([got[d] for d in got if d & PAIR])
-        low = jnp.where(side == 0, near, pair).reshape(chunk, EXPERTS, hidden)
-        high = jnp.where(side == 0, pair, near).reshape(chunk, EXPERTS, hidden)
-        return jnp.swapaxes(jnp.concatenate([low, high], axis=2), 0, 1)
-
     got_down = collect(down_even, down_odd, n)
     got_gate = collect(gate_even, gate_odd, n)
     got_up = collect(up_even, up_odd, n)
@@ -640,17 +656,17 @@
         [((count, q_cols), BF), ((n // 2, chunk, q_cols), BF), ((n // 2, chunk, q_cols), BF)],
         [pltpu.VMEM((D, q_cols), BF), pltpu.VMEM((count, D), BF), dma((n,))],
         [SMEM] * 2 + [VMEM] * 4 + [ANY] * n + [VMEM],
-        [owners, me, *da, *attn_w, mixed],
+        [owners, me, *da, *out_w, mixed],
         1.2e9, 4e6,
     )
     got_out = collect(out_even, out_odd, n)
-    dqkv, q_even, q_odd, kv_even, kv_odd, grad_norm1 = call(
+    dqkv, q_even, q_odd, kv_even, kv_odd = call(
         functools.partial(attend_back_kernel, n, heads),
-        [((count, qkv_cols), BF)] + [((n // 2, chunk, q_cols), BF)] * 2
-        + [((n // 2, chunk, 2 * kv_cols), BF)] * 2 + [((8, D), F32)],
+        [((count, qkv_cols), BF)] + [((n // 2, chunk + EXTRA, q_cols), BF)] * 2
+        + [((n // 2, chunk, 2 * kv_cols), BF)] * 2,
         [pltpu.VMEM((D, qkv_cols), BF), dma((n,))],
-        [SMEM] * 2 + [ANY] * n + [VMEM] * 4,
-        [owners, me, *attn_w, n1, qkv, do, bias],
+        [SMEM] * 2 + [ANY] * n + [VMEM] * 6,
+        [owners, me, *qkv_w, n1, qkv, do, probs, grad_norm2, grad_router],
         8e9, 5e6,
     )
     sum_q = total(list(collect(q_even, q_odd, n).values()))
@@ -660,44 +676,51 @@
         [block] * 4,
         [pltpu.VMEM((D, qkv_cols), BF), dma((n,))],
         [SMEM] + [ANY] * n + [VMEM],
-        [owners, *attn_w, dqkv],
+        [owners, *qkv_w, dqkv],
         1e9, 6e6,
     )
-    got_down, got_gate, got_up, got_out, _ = lax.optimization_barrier(
-        (got_down, got_gate, got_up, got_out, part[0])
-    )
-    sum_down = jnp.swapaxes(share(got_down), 1, 2)
-    sum_gate, sum_up = share(got_gate), share(got_up)
-    sum_out = total(list(got_out.values())).T
     (grad_input,) = call(
         input_kernel, [((own, D), F32)], [], [VMEM] * 6,
         [x_own, *seq_scatter(part), dh, small], 0, 3e6,
     )
-    y_parts = wide_scatter(y_near, y_away)
-    layer_out = total([h, y_parts[0][0], y_parts[1][0], *y_parts[2:]]).astype(BF)
-
-    tiny = jnp.concatenate([grad_norm1[:1], grad_norm2, grad_router[:4], jnp.zeros((2, D), F32)], axis=0)
-    for bit in range(n.bit_length() - 1):
-        tiny = tiny + move(tiny, "fsdp", 1 << bit)
-    tiny = lax.dynamic_slice_in_dim(tiny, mine * chunk, chunk, axis=1)
-    for bit in (2, 1):
-        tiny = tiny + move(tiny, "seq", bit)
+    ins = []
+    for got in (got_down, got_gate, got_up):
+        ins.append([got[d] for d in got if not d & PAIR] + [got[d] for d in got if d & PAIR])
+    ins.append(list(got_out.values()))
+    sum_down, sum_gate, sum_up, sum_out = call(
+        functools.partial(finish_kernel, [len(v) for v in ins], hidden),
+        [((EXPERTS, chunk, 2 * hidden), F32)] * 3 + [((chunk, q_cols), F32)], [],
+        [SMEM] + [VMEM] * sum(len(v) for v in ins),
+        [side.reshape(1).astype(jnp.int32)] + [v for part in ins for v in part], 0, 6e6,
+    )
+    y_away = move(y_away, "seq", 1)
+    far = move(add(y_near[1::2], y_away[1::2]), "seq", 2)
+    pair = move(total([y_near[2], y_away[2], far[1]]).astype(BF), "fsdp", PAIR)
+    layer_out = total([h, y_near[0], y_away[0], far[0], pair]).astype(BF)
+
+    tiny = sum_q[chunk : chunk + 8, :chunk]
+    tiny = tiny + move(tiny, "seq", 2)
+    tiny = tiny + move(tiny, "seq", 1)
 
     lead = (micro, 1, rows, D)
     return (
         layer_out.reshape(lead),
         grad_input.reshape(lead),
         tiny[0] / norm1.astype(F32),
-        sum_q,
+        sum_q[:chunk],
         sum_kv[:, :kv_cols],
         sum_kv[:, kv_cols:],
-        sum_out,
+        sum_out.T,
         tiny[1],
         tiny[2:6].T,
         sum_gate,
         sum_up,
-        sum_down,
-    )
+        jnp.swapaxes(sum_down, 1, 2),
+    )
+
+
+def directions(n):
+    return sorted(range(2, n, 2), key=lambda d: (d & (d - 1) != 0, -d))
 
 
 def solution(mesh):

time: 411 us -> 429 us (1.044); the launches traced: 405 us -> 428 us
  starting transfers between devices: 92.7 us -> 120 us
  other arithmetic: 14.7 us -> 10.2 us
    ppermute x76 -> x80, starting transfers between devices: 89.2 us -> 118 us  [move(): lax.ppermute(value, axis, [(i, i ^ bit) for i in range(lax.axis_size(axis...]
    ppermute x2 -> x1, waiting for transfers between devices: 5.88 us -> 0.01 us  [move_both(): return lax.ppermute(value, ('seq', 'fsdp'), pairs)]
    ppermute x76 -> x80, waiting for transfers between devices: 190 us -> 196 us  [move(): lax.ppermute(value, axis, [(i, i ^ bit) for i in range(lax.axis_size(axis...]
    pallas_call x13 -> x14, Pallas kernels: 88.9 us -> 86.7 us  [call(): pl.pallas_call(kernel, grid=grid, in_specs=specs, out_specs=out_specs or...]
  transfers between devices with their start and end apart: 78 -> 81, of which waited for: 26 -> 30; matrix products, arithmetic and copies ran while one was open for 5% -> 4% of each run, Pallas kernels for 14% -> 14%
where the time goes in v1:
time: 429 us; the launch traced here: 428 us
  waiting for transfers between devices  196 us (46%)
  starting transfers between devices  120 us (28%)
  Pallas kernels  86.7 us (20%)
  local copies, waits for them, and re-layouts  13.7 us (3%)
  other arithmetic  10.2 us (2%)
    ppermute x80, waiting for transfers between devices, move(): lax.ppermute(value, axis, [(i, i ^ bit) for i in range(lax.axis_size(axis...  196 us
    ppermute x80, starting transfers between devices, move(): lax.ppermute(value, axis, [(i, i ^ bit) for i in range(lax.axis_size(axis...  118 us
    pallas_call x14, Pallas kernels, call(): pl.pallas_call(kernel, grid=grid, in_specs=specs, out_specs=out_specs or...  86.7 us
  transfers between devices with their start and end apart: 81, of which 30 were waited for; matrix products, arithmetic and copies ran while one was open for 4% of the time, Pallas kernels for 14%

profile of v1, /device:TPU:0, one launch (start us, length us, event | category | flops | bytes accessed | tf_op | source)
XLA Modules:
  0.0 427.9 jit_solution(6083596243371479630)
XLA Ops:
  18.3 12.5 %collective-permute-done.3.refs_4_.refs_8_ = bf16[192,384]{1,0:T(8,128)(2,1)S(1)} collective-permute-done((bf16[192,384]{1,0:T(8,128)(2,1)}, bf16[192,384]{1,0:T(8,128)(2,1)S(1)}, u32[]{:S(2)}, u32[]{:S(2)}) %collective-permute-start.3) | collective-permute-done | bytes 147488 | tf_op jit(solution)/shard_map/ppermute | solution.py:37
  34.3 7.1 %collective-permute-done.13.refs_8_.refs_4_ = bf16[208,640]{1,0:T(8,128)(2,1)S(1)} collective-permute-done((bf16[208,640]{1,0:T(8,128)(2,1)}, bf16[208,640]{1,0:T(8,128)(2,1)S(1)}, u32[]{:S(2)}, u32[]{:S(2)}) %collective-permute-start.13) | collective-permute-done | bytes 266272 | tf_op jit(solution)/shard_map/ppermute | solution.py:37
  64.9 5.8 %shard_map.230 = (bf16[512,1536]{1,0:T(8,128)(2,1)}, bf16[512,640]{1,0:T(8,128)(2,1)}, f32[16,1536]{1,0:T(8,128)}) custom-call(s32[8]{0:T(128)} %iota_xor_fusion.1.owners, bf16[128,1536]{1,0:T(8,128)(2,1)} %bitcast.135, bf16[128,1536]{1,0:T(8,128)(2,1)} %copy-done.17, bf16[128,1536]{1,0:T(8,128)(2,1)} %copy-done.16, bf16[128,1536]{1,0:T(8,128)(2,1)} %copy-done.18, ...), custom_call_target="tpu_custom_call" | custom-call | flops 1000000000 | bytes 6000000 | tf_op jit(solution)/shard_map/pallas_call | solution.py:114
  73.5 6.4 %shard_map.231 = (bf16[512,384]{1,0:T(8,128)(2,1)}, bf16[12,256,256]{2,1,0:T(8,128)(2,1)}, bf16[128,1536]{1,0:T(8,128)(2,1)}, bf16[128,1536]{1,0:T(8,128)(2,1)},...) custom-call(s32[8]{0:T(128)} %iota_xor_fusion.1.owners, bf16[192,384]{1,0:T(8,128)(2,1)} %bitcast.162, ...), custom_call_target="tpu_custom_call" | custom-call | flops 5000000000 | bytes 6000000 | tf_op jit(solution)/shard_map/pallas_call | solution.py:114
  92.5 14.0 %collective-permute-start.23 = (bf16[192,1536]{1,0:T(8,128)(2,1)}, bf16[192,1536]{1,0:T(8,128)(2,1)}, u32[]{:S(2)}, u32[]{:S(2)}) collective-permute-start(bf16[192,1536]{1,0:T(8,128)(2,1)} %get-tuple-element.64.refs_16_.refs_0_), channel_id=1, source_target_pairs={{0,4},{1,5},{2,6},{3,7},{4,0},{5,1},{6,2},{7,3},{8,12},{9,13},{10,... | collective-permute-start | bytes 1769480 | tf_op jit(solution)/shard_map/ppermute | solution.py:37
  111.6 6.8 %collective-permute-done.19.c_ref = bf16[128,1536]{1,0:T(8,128)(2,1)S(1)} collective-permute-done((bf16[128,1536]{1,0:T(8,128)(2,1)S(1)}, bf16[128,1536]{1,0:T(8,128)(2,1)S(1)}, u32[]{:S(2)}, u32[]{:S(2)}) %collective-permute-start.19) | collective-permute-done | bytes 393248 | tf_op jit(solution)/shard_map/ppermute | solution.py:37
  122.8 16.8 %collective-permute-done.23.refs_20_.refs_4_ = bf16[192,1536]{1,0:T(8,128)(2,1)} collective-permute-done((bf16[192,1536]{1,0:T(8,128)(2,1)}, bf16[192,1536]{1,0:T(8,128)(2,1)}, u32[]{:S(2)}, u32[]{:S(2)}) %collective-permute-start.23) | collective-permute-done | bytes 589856 | tf_op jit(solution)/shard_map/ppermute | solution.py:37
  142.3 7.2 %collective-permute-done.28.refs_2_ = bf16[128,1536]{1,0:T(8,128)(2,1)S(1)} collective-permute-done((bf16[128,1536]{1,0:T(8,128)(2,1)}, bf16[128,1536]{1,0:T(8,128)(2,1)S(1)}, u32[]{:S(2)}, u32[]{:S(2)}) %collective-permute-start.28) | collective-permute-done | bytes 393248 | tf_op jit(solution)/shard_map/ppermute | solution.py:37
  155.9 12.6 %collective-permute-done.22.refs_19_.refs_3_ = bf16[192,1536]{1,0:T(8,128)(2,1)S(1)} collective-permute-done((bf16[192,1536]{1,0:T(8,128)(2,1)}, bf16[192,1536]{1,0:T(8,128)(2,1)S(1)}, u32[]{:S(2)}, u32[]{:S(2)}) %collective-permute-start.22) | collective-permute-done | bytes 589856 | tf_op jit(solution)/shard_map/ppermute | solution.py:37
  172.2 6.7 %collective-permute-done.24.refs_21_.refs_5_ = bf16[192,1536]{1,0:T(8,128)(2,1)S(1)} collective-permute-done((bf16[192,1536]{1,0:T(8,128)(2,1)}, bf16[192,1536]{1,0:T(8,128)(2,1)S(1)}, u32[]{:S(2)}, u32[]{:S(2)}) %collective-permute-start.24) | collective-permute-done | bytes 589856 | tf_op jit(solution)/shard_map/ppermute | solution.py:37
  179.7 19.2 %shard_map.234 = (bf16[1024,512]{1,0:T(8,128)(2,1)}, bf16[1024,1152]{1,0:T(8,128)(2,1)}, bf16[4,128,1536]{2,1,0:T(8,128)(2,1)}, bf16[4,128,1536]{2,1,0:T(8,128)(...) custom-call(s32[8]{0:T(128)} %iota_xor_fusion.1.owners, s32[1]{0:T(128)} %bitcast.7.mine, ...), custom_call_target="tpu_custom_call" | custom-call | flops 10000000000 | bytes 20000000 | tf_op jit(solution)/shard_map/pallas_call | solution.py:114
  199.0 5.8 %shard_map.235 = (bf16[4,128,1536]{2,1,0:T(8,128)(2,1)}, bf16[4,128,1536]{2,1,0:T(8,128)(2,1)}) custom-call(s32[8]{0:T(128)} %iota_xor_fusion.1.owners, bf16[192,1536]{1,0:T(8,128)(2,1)} %get-tuple-element.64.refs_16_.refs_0_, bf16[192,1536]{1,0:T(8,128)(2,1)} %copy-done.50, bf16[192,1536]{1,0:T(8,128)(2,1)} %collective-permute-done.21.refs_18_.refs_2_, ...), custom_call_target="tpu_custom_call" | custom-call | flops 1600000000 | bytes 6000000 | tf_op jit(solution)/shard_map/pallas_call | solution.py:114
  205.4 9.9 %shard_map.238 = (bf16[4,192,512]{2,1,0:T(8,128)(2,1)}, bf16[4,192,512]{2,1,0:T(8,128)(2,1)}, bf16[4,192,512]{2,1,0:T(8,128)(2,1)}, bf16[4,192,512]{2,1,0:T(8,128)(2,1)}, f32[8,1536]{1,0:T(8,128)}) custom-call(s32[1]{0:T(128)} %bitcast.7.mine, bf16[128,1536]{1,0:T(8,128)(2,1)} %get-tuple-element.66.refs_0_, ...), custom_call_target="tpu_custom_call" | custom-call | flops 3500000000 | bytes 9000000 | tf_op jit(solution)/shard_map/pallas_call | solution.py:114
  221.7 14.3 %collective-permute-done.69 = bf16[4,192,512]{2,1,0:T(8,128)(2,1)S(1)} collective-permute-done((bf16[4,192,512]{2,1,0:T(8,128)(2,1)}, bf16[4,192,512]{2,1,0:T(8,128)(2,1)S(1)}, u32[]{:S(2)}, u32[]{:S(2)}) %collective-permute-start.69) | collective-permute-done | bytes 786464 | tf_op jit(solution)/shard_map/ppermute | solution.py:37
  255.6 13.1 %collective-permute-done.65 = bf16[4,192,512]{2,1,0:T(8,128)(2,1)S(1)} collective-permute-done((bf16[4,192,512]{2,1,0:T(8,128)(2,1)}, bf16[4,192,512]{2,1,0:T(8,128)(2,1)S(1)}, u32[]{:S(2)}, u32[]{:S(2)}) %collective-permute-start.65) | collective-permute-done | bytes 786464 | tf_op jit(solution)/shard_map/ppermute | solution.py:37
  279.5 12.1 %shard_map.239 = (bf16[512,640]{1,0:T(8,128)(2,1)}, bf16[4,208,384]{2,1,0:T(8,128)(2,1)}, bf16[4,208,384]{2,1,0:T(8,128)(2,1)}, bf16[4,192,256]{2,1,0:T(8,128)(2,1)}, bf16[4,192,256]{2,1,0:T(8,128)(2,1)}) custom-call(s32[8]{0:T(128)} %iota_xor_fusion.1.owners, s32[1]{0:T(128)} %bitcast.7.mine, bf16[208,640]{1,0:T(8,128)(2,1)} %shard_map.229.refs_4_.refs_0_, ...), custom_call_target="tpu_custom_call" | custom-call | flops 8000000000 | bytes 5000000 | tf_op jit(solution)/shard_map/pallas_call | solution.py:114
  301.8 7.5 %collective-permute-done.61 = bf16[4,192,256]{2,1,0:T(8,128)(2,1)S(1)} collective-permute-done((bf16[4,192,256]{2,1,0:T(8,128)(2,1)S(1)}, bf16[4,192,256]{2,1,0:T(8,128)(2,1)S(1)}, u32[]{:S(2)}, u32[]{:S(2)}) %collective-permute-start.61) | collective-permute-done | bytes 393248 | tf_op jit(solution)/shard_map/ppermute | solution.py:37
  311.9 23.1 %collective-permute-done.55 = bf16[4,208,384]{2,1,0:T(8,128)(2,1)S(1)} collective-permute-done((bf16[4,208,384]{2,1,0:T(8,128)(2,1)S(1)}, bf16[4,208,384]{2,1,0:T(8,128)(2,1)S(1)}, u32[]{:S(2)}, u32[]{:S(2)}) %collective-permute-start.55) | collective-permute-done | bytes 639008 | tf_op jit(solution)/shard_map/ppermute | solution.py:37
  338.7 7.4 %collective-permute-done.63 = bf16[192,256]{1,0:T(8,128)(2,1)S(1)} collective-permute-done((bf16[192,256]{1,0:T(8,128)(2,1)S(1)}, bf16[192,256]{1,0:T(8,128)(2,1)S(1)}, u32[]{:S(2)}, u32[]{:S(2)}) %collective-permute-start.63) | collective-permute-done | bytes 98336 | tf_op jit(solution)/shard_map/ppermute | solution.py:37
  348.6 10.6 %collective-permute-start.70 = (bf16[192,512]{1,0:T(8,128)(2,1)S(1)}, bf16[192,512]{1,0:T(8,128)(2,1)S(1)}, u32[]{:S(2)}, u32[]{:S(2)}) collective-permute-start(bf16[192,512]{1,0:T(8,128)(2,1)S(1)} %copy-done.30), channel_id=1, source_target_pairs={{0,4},{1,5},{2,6},{3,7},{4,0},{5,1},{6,2},{7,3},{8,12},{9,13},{10,... | collective-permute-start | bytes 589832 | tf_op jit(solution)/shard_map/ppermute | solution.py:37
  365.6 9.0 %collective-permute-start.74 = (bf16[192,512]{1,0:T(8,128)(2,1)S(1)}, bf16[192,512]{1,0:T(8,128)(2,1)S(1)}, u32[]{:S(2)}, u32[]{:S(2)}) collective-permute-start(bf16[192,512]{1,0:T(8,128)(2,1)S(1)} %get-tuple-element.143), channel_id=1, source_target_pairs={{0,4},{1,5},{2,6},{3,7},{4,0},{5,1},{6,2},{7,3},{8,12},{9,13},{10,... | collective-permute-start | bytes 589832 | tf_op jit(solution)/shard_map/ppermute | solution.py:37
  374.6 7.2 %collective-permute-done.70.refs_5_ = bf16[192,512]{1,0:T(8,128)(2,1)S(1)} collective-permute-done((bf16[192,512]{1,0:T(8,128)(2,1)S(1)}, bf16[192,512]{1,0:T(8,128)(2,1)S(1)}, u32[]{:S(2)}, u32[]{:S(2)}) %collective-permute-start.70) | collective-permute-done | bytes 196640 | tf_op jit(solution)/shard_map/ppermute | solution.py:37
  387.3 11.4 %collective-permute-done.74.refs_9_ = bf16[192,512]{1,0:T(8,128)(2,1)S(1)} collective-permute-done((bf16[192,512]{1,0:T(8,128)(2,1)S(1)}, bf16[192,512]{1,0:T(8,128)(2,1)S(1)}, u32[]{:S(2)}, u32[]{:S(2)}) %collective-permute-start.74) | collective-permute-done | bytes 196640 | tf_op jit(solution)/shard_map/ppermute | solution.py:37
  404.2 6.1 %collective-permute-done.66.refs_1_ = bf16[192,512]{1,0:T(8,128)(2,1)S(1)} collective-permute-done((bf16[192,512]{1,0:T(8,128)(2,1)S(1)}, bf16[192,512]{1,0:T(8,128)(2,1)S(1)}, u32[]{:S(2)}, u32[]{:S(2)}) %collective-permute-start.66) | collective-permute-done | bytes 196640 | tf_op jit(solution)/shard_map/ppermute | solution.py:37
  (356 shorter events, 173.7 us)
Async XLA Ops:
  8.1 26.1 %collective-permute-start.15 = (bf16[208,640]{1,0:T(8,128)(2,1)}, bf16[208,640]{1,0:T(8,128)(2,1)S(1)}, u32[]{:S(2)}, u32[]{:S(2)}) collective-permute-start(bf16[208,640]{1,0:T(8,128)(2,1)} %shard_map.229.refs_4_.refs_0_), channel_id=1, source_target_pairs={{0,6},{1,7},{2,4},{3,5},{4,2},{5,3},{6,0},{7,1},{8,14},{9,15},{10,... | collective-permute-start | bytes 798728 | tf_op jit(solution)/shard_map/ppermute | solution.py:37
  11.9 33.4 %collective-permute-start.8 = (bf16[128,1536]{1,0:T(8,128)(2,1)}, bf16[128,1536]{1,0:T(8,128)(2,1)S(1)}, u32[]{:S(2)}, u32[]{:S(2)}) collective-permute-start(bf16[128,1536]{1,0:T(8,128)(2,1)} %bitcast.133), channel_id=1, source_target_pairs={{0,16},{8,24},{16,0},{24,8},{1,17},{9,25},{17,1},{25,9},{2,18},{10... | collective-permute-start | bytes 1179656 | tf_op jit(solution)/shard_map/ppermute | solution.py:37
  13.5 27.9 %collective-permute-start.13 = (bf16[208,640]{1,0:T(8,128)(2,1)}, bf16[208,640]{1,0:T(8,128)(2,1)S(1)}, u32[]{:S(2)}, u32[]{:S(2)}) collective-permute-start(bf16[208,640]{1,0:T(8,128)(2,1)} %shard_map.229.refs_4_.refs_0_), channel_id=1, source_target_pairs={{0,4},{1,5},{2,6},{3,7},{4,0},{5,1},{6,2},{7,3},{8,12},{9,13},{10,... | collective-permute-start | bytes 798728 | tf_op jit(solution)/shard_map/ppermute | solution.py:37
  80.5 25.9 %collective-permute-start.35 = (bf16[128,1536]{1,0:T(8,128)(2,1)S(1)}, bf16[128,1536]{1,0:T(8,128)(2,1)}, u32[]{:S(2)}, u32[]{:S(2)}) collective-permute-start(bf16[128,1536]{1,0:T(8,128)(2,1)S(1)} %bitcast.144), channel_id=1, source_target_pairs={{0,2},{1,3},{2,0},{3,1},{4,6},{5,7},{6,4},{7,5},{8,10},{9,11},{10,... | collective-permute-start | bytes 1179656 | tf_op jit(solution)/shard_map/ppermute | solution.py:37
  80.5 25.9 %collective-permute-start.34 = (bf16[128,1536]{1,0:T(8,128)(2,1)S(1)}, bf16[128,1536]{1,0:T(8,128)(2,1)}, u32[]{:S(2)}, u32[]{:S(2)}) collective-permute-start(bf16[128,1536]{1,0:T(8,128)(2,1)S(1)} %bitcast.145), channel_id=1, source_target_pairs={{0,16},{8,24},{16,0},{24,8},{1,17},{9,25},{17,1},{25,9},{2,18},{10... | collective-permute-start | bytes 1179656 | tf_op jit(solution)/shard_map/ppermute | solution.py:37
  91.8 31.0 %collective-permute-start.21 = (bf16[192,1536]{1,0:T(8,128)(2,1)}, bf16[192,1536]{1,0:T(8,128)(2,1)}, u32[]{:S(2)}, u32[]{:S(2)}) collective-permute-start(bf16[192,1536]{1,0:T(8,128)(2,1)} %get-tuple-element.65), channel_id=1, source_target_pairs={{0,2},{1,3},{2,0},{3,1},{4,6},{5,7},{6,4},{7,5},{8,10},{9,11},{10,... | collective-permute-start | bytes 1769480 | tf_op jit(solution)/shard_map/ppermute | solution.py:37
  92.5 47.1 %collective-permute-start.23 = (bf16[192,1536]{1,0:T(8,128)(2,1)}, bf16[192,1536]{1,0:T(8,128)(2,1)}, u32[]{:S(2)}, u32[]{:S(2)}) collective-permute-start(bf16[192,1536]{1,0:T(8,128)(2,1)} %get-tuple-element.64.refs_16_.refs_0_), channel_id=1, source_target_pairs={{0,4},{1,5},{2,6},{3,7},{4,0},{5,1},{6,2},{7,3},{8,12},{9,13},{10,... | collective-permute-start | bytes 1769480 | tf_op jit(solution)/shard_map/ppermute | solution.py:37
  110.0 29.6 %collective-permute-start.20 = (bf16[192,1536]{1,0:T(8,128)(2,1)S(1)}, bf16[192,1536]{1,0:T(8,128)(2,1)S(1)}, u32[]{:S(2)}, u32[]{:S(2)}) collective-permute-start(bf16[192,1536]{1,0:T(8,128)(2,1)S(1)} %copy-done.47), channel_id=1, source_target_pairs={{0,1},{1,0},{2,3},{3,2},{4,5},{5,4},{6,7},{7,6},{8,9},{9,8},{10,11... | collective-permute-start | bytes 1769480 | tf_op jit(solution)/shard_map/ppermute | solution.py:37
  111.6 29.7 %collective-permute-start.39 = (bf16[128,1536]{1,0:T(8,128)(2,1)}, bf16[128,1536]{1,0:T(8,128)(2,1)S(1)}, u32[]{:S(2)}, u32[]{:S(2)}) collective-permute-start(bf16[128,1536]{1,0:T(8,128)(2,1)} %collective-permute-done.35.refs_10_), channel_id=1, source_target_pairs={{0,8},{8,0},{16,24},{24,16},{1,9},{9,1},{17,25},{25,17},{2,10},{10... | collective-permute-start | bytes 1179656 | tf_op jit(solution)/shard_map/ppermute | solution.py:37
  141.2 27.3 %collective-permute-start.22 = (bf16[192,1536]{1,0:T(8,128)(2,1)}, bf16[192,1536]{1,0:T(8,128)(2,1)S(1)}, u32[]{:S(2)}, u32[]{:S(2)}) collective-permute-start(bf16[192,1536]{1,0:T(8,128)(2,1)} %collective-permute-done.21.refs_18_.refs_2_), channel_id=1, source_target_pairs={{0,1},{1,0},{2,3},{3,2},{4,5},{5,4},{6,7},{7,6},{8,9},{9,8},{10,11... | collective-permute-start | bytes 1769480 | tf_op jit(solution)/shard_map/ppermute | solution.py:37
  141.8 26.8 %collective-permute-start.27 = (bf16[128,1536]{1,0:T(8,128)(2,1)}, bf16[128,1536]{1,0:T(8,128)(2,1)}, u32[]{:S(2)}, u32[]{:S(2)}) collective-permute-start(bf16[128,1536]{1,0:T(8,128)(2,1)} %get-tuple-element.66.refs_0_), channel_id=1, source_target_pairs={{0,16},{8,24},{16,0},{24,8},{1,17},{9,25},{17,1},{25,9},{2,18},{10... | collective-permute-start | bytes 1179656 | tf_op jit(solution)/shard_map/ppermute | solution.py:37
  150.1 28.7 %collective-permute-start.24 = (bf16[192,1536]{1,0:T(8,128)(2,1)}, bf16[192,1536]{1,0:T(8,128)(2,1)S(1)}, u32[]{:S(2)}, u32[]{:S(2)}) collective-permute-start(bf16[192,1536]{1,0:T(8,128)(2,1)} %collective-permute-done.23.refs_20_.refs_4_), channel_id=1, source_target_pairs={{0,1},{1,0},{2,3},{3,2},{4,5},{5,4},{6,7},{7,6},{8,9},{9,8},{10,11... | collective-permute-start | bytes 1769480 | tf_op jit(solution)/shard_map/ppermute | solution.py:37
  204.8 32.9 %collective-permute-start.42 = (bf16[4,128,1536]{2,1,0:T(8,128)(2,1)}, bf16[4,128,1536]{2,1,0:T(8,128)(2,1)S(1)}, u32[]{:S(2)}, u32[]{:S(2)}) collective-permute-start(bf16[4,128,1536]{2,1,0:T(8,128)(2,1)} %get-tuple-element.69), channel_id=1, source_target_pairs={{0,8},{8,0},{16,24},{24,16},{1,9},{9,1},{17,25},{25,17},{2,10},{10... | collective-permute-start | bytes 4718600 | tf_op jit(solution)/shard_map/ppermute | solution.py:37
  216.9 37.7 %collective-permute-start.73 = (bf16[4,192,512]{2,1,0:T(8,128)(2,1)}, bf16[4,192,512]{2,1,0:T(8,128)(2,1)S(1)}, u32[]{:S(2)}, u32[]{:S(2)}) collective-permute-start(bf16[4,192,512]{2,1,0:T(8,128)(2,1)} %get-tuple-element.95), channel_id=1, source_target_pairs={{0,1},{1,0},{2,3},{3,2},{4,5},{5,4},{6,7},{7,6},{8,9},{9,8},{10,11... | collective-permute-start | bytes 2359304 | tf_op jit(solution)/shard_map/ppermute | solution.py:37
  217.4 51.4 %collective-permute-start.65 = (bf16[4,192,512]{2,1,0:T(8,128)(2,1)}, bf16[4,192,512]{2,1,0:T(8,128)(2,1)S(1)}, u32[]{:S(2)}, u32[]{:S(2)}) collective-permute-start(bf16[4,192,512]{2,1,0:T(8,128)(2,1)} %get-tuple-element.91), channel_id=1, source_target_pairs={{0,1},{1,0},{2,3},{3,2},{4,5},{5,4},{6,7},{7,6},{8,9},{9,8},{10,11... | collective-permute-start | bytes 2359304 | tf_op jit(solution)/shard_map/ppermute | solution.py:37
  238.4 33.5 %collective-permute-start.43 = (bf16[2,128,1536]{2,1,0:T(8,128)(2,1)S(1)}, bf16[2,128,1536]{2,1,0:T(8,128)(2,1)S(1)}, u32[]{:S(2)}, u32[]{:S(2)}) collective-permute-start(bf16[2,128,1536]{2,1,0:T(8,128)(2,1)S(1)} %add_convert_fusion), channel_id=1, source_target_pairs={{0,16},{8,24},{16,0},{24,8},{1,17},{9,25},{17,1},{25,9},{2,18},{10... | collective-permute-start | bytes 2359304 | tf_op jit(solution)/shard_map/ppermute | solution.py:37
  245.2 117.0 %collective-permute-start.72 = (bf16[192,512]{1,0:T(8,128)(2,1)}, bf16[192,512]{1,0:T(8,128)(2,1)}, u32[]{:S(2)}, u32[]{:S(2)}) collective-permute-start(bf16[192,512]{1,0:T(8,128)(2,1)} %get-tuple-element.145), channel_id=1, source_target_pairs={{0,2},{1,3},{2,0},{3,1},{4,6},{5,7},{6,4},{7,5},{8,10},{9,11},{10,... | collective-permute-start | bytes 589832 | tf_op jit(solution)/shard_map/ppermute | solution.py:37
  272.1 26.6 %collective-permute-start.44 = (bf16[128,1536]{1,0:T(8,128)(2,1)S(1)}, bf16[128,1536]{1,0:T(8,128)(2,1)S(1)}, u32[]{:S(2)}, u32[]{:S(2)}) collective-permute-start(bf16[128,1536]{1,0:T(8,128)(2,1)S(1)} %fusion.4), channel_id=1, source_target_pairs={{0,2},{1,3},{2,0},{3,1},{4,6},{5,7},{6,4},{7,5},{8,10},{9,11},{10,... | collective-permute-start | bytes 1179656 | tf_op jit(solution)/shard_map/ppermute | solution.py:37
  299.7 82.0 %collective-permute-start.77 = (bf16[4,192,384]{2,1,0:T(8,128)(2,1)S(1)}, bf16[4,192,384]{2,1,0:T(8,128)(2,1)S(1)}, u32[]{:S(2)}, u32[]{:S(2)}) collective-permute-start(bf16[4,192,384]{2,1,0:T(8,128)(2,1)S(1)} %copy-done.49), channel_id=1, source_target_pairs={{0,1},{1,0},{2,3},{3,2},{4,5},{5,4},{6,7},{7,6},{8,9},{9,8},{10,11... | collective-permute-start | bytes 1769480 | tf_op jit(solution)/shard_map/ppermute | solution.py:37
  300.3 34.7 %collective-permute-start.55 = (bf16[4,208,384]{2,1,0:T(8,128)(2,1)S(1)}, bf16[4,208,384]{2,1,0:T(8,128)(2,1)S(1)}, u32[]{:S(2)}, u32[]{:S(2)}) collective-permute-start(bf16[4,208,384]{2,1,0:T(8,128)(2,1)S(1)} %copy-done.46), channel_id=1, source_target_pairs={{0,1},{1,0},{2,3},{3,2},{4,5},{5,4},{6,7},{7,6},{8,9},{9,8},{10,11... | collective-permute-start | bytes 1916936 | tf_op jit(solution)/shard_map/ppermute | solution.py:37
  309.3 27.3 %collective-permute-start.62 = (bf16[192,256]{1,0:T(8,128)(2,1)S(1)}, bf16[192,256]{1,0:T(8,128)(2,1)S(1)}, u32[]{:S(2)}, u32[]{:S(2)}) collective-permute-start(bf16[192,256]{1,0:T(8,128)(2,1)S(1)} %get-tuple-element.160), channel_id=1, source_target_pairs={{0,6},{1,7},{2,4},{3,5},{4,2},{5,3},{6,0},{7,1},{8,14},{9,15},{10,... | collective-permute-start | bytes 294920 | tf_op jit(solution)/shard_map/ppermute | solution.py:37
  311.7 26.5 %collective-permute-start.64 = (bf16[192,256]{1,0:T(8,128)(2,1)S(1)}, bf16[192,256]{1,0:T(8,128)(2,1)S(1)}, u32[]{:S(2)}, u32[]{:S(2)}) collective-permute-start(bf16[192,256]{1,0:T(8,128)(2,1)S(1)} %get-tuple-element.161), channel_id=1, source_target_pairs={{0,2},{1,3},{2,0},{3,1},{4,6},{5,7},{6,4},{7,5},{8,10},{9,11},{10,... | collective-permute-start | bytes 294920 | tf_op jit(solution)/shard_map/ppermute | solution.py:37
  348.6 33.2 %collective-permute-start.70 = (bf16[192,512]{1,0:T(8,128)(2,1)S(1)}, bf16[192,512]{1,0:T(8,128)(2,1)S(1)}, u32[]{:S(2)}, u32[]{:S(2)}) collective-permute-start(bf16[192,512]{1,0:T(8,128)(2,1)S(1)} %copy-done.30), channel_id=1, source_target_pairs={{0,4},{1,5},{2,6},{3,7},{4,0},{5,1},{6,2},{7,3},{8,12},{9,13},{10,... | collective-permute-start | bytes 589832 | tf_op jit(solution)/shard_map/ppermute | solution.py:37
  365.6 33.1 %collective-permute-start.74 = (bf16[192,512]{1,0:T(8,128)(2,1)S(1)}, bf16[192,512]{1,0:T(8,128)(2,1)S(1)}, u32[]{:S(2)}, u32[]{:S(2)}) collective-permute-start(bf16[192,512]{1,0:T(8,128)(2,1)S(1)} %get-tuple-element.143), channel_id=1, source_target_pairs={{0,4},{1,5},{2,6},{3,7},{4,0},{5,1},{6,2},{7,3},{8,12},{9,13},{10,... | collective-permute-start | bytes 589832 | tf_op jit(solution)/shard_map/ppermute | solution.py:37
  (126 other events, 1971.6 us)
